TPU v7x, 32 devices: a whole 2x2x4 slice. The times are simulated.
32 devices in a mesh: coarse: 8 (over z, y), fine: 4 (over x, core).
Axes of the slice: x: 2, y: 2, z: 4, core: 2. Of those that a mesh axis runs over, the one named last changes fastest.
Arguments:
- right_side: float32 [64, 32, 128], P('coarse', 'fine'), may hold values from -6 to 6
- coefficient_index: int32 [64, 32, 128], P('coarse', 'fine'), may hold values from 0 to 15
- material_coefficients: float32 [16], replicated, may hold values from 0.02 to 0.5
- block_cells: int32 [8, 4, 64, 128], P('coarse', 'fine'), may hold values from 0 to 8191, as said below
- block_inverses: float32 [8, 4, 64, 128, 128], P('coarse', 'fine'), as said below
- aggregate_map: int32 [64, 32, 128], P('coarse', 'fine'), may hold values from 0 to 15, as said below
- coarse_diagonal: float32 [8, 4, 16], P('coarse', 'fine'), may hold values from 0.1 to 8
Outputs:
- solution: float32 [64, 32, 128], P('coarse', 'fine')
- residual: float32 [64, 32, 128], P('coarse', 'fine')
- direction: float32 [64, 32, 128], P('coarse', 'fine')
Inputs may be any that keep to these rules, and one draw needn't show every extreme that they name: `block_cells`: each device block's 64 x 128 entries list each of its local cell numbers exactly once. `block_inverses`: every 128 x 128 matrix is symmetric positive definite. A cell with third index j has aggregate_map equal to j // 8 - 1, j // 8 or j // 8 + 1.
All inputs are finite; a program needn't handle non-finite values.
Results may differ from a plain program's by a relative error of at most 0.00016.
Values sent between devices are 32-bit elements; how exact they have to be, the bound alone decides.
A program may use at most 64 MiB of HBM per device.

v0:
```python
import functools

import jax
import jax.numpy as jnp
from jax import lax
from jax.experimental import pallas as pl
from jax.experimental.pallas import tpu as pltpu
from jax.sharding import PartitionSpec as P

ITERS = 2
SWEEPS = 4
omega = 0.8
restrict_scale = 0.25
MESH = pl.DeviceIdType.MESH
SUB = 8
LANES = 128
MAIN = 8
XLO, XHI, ZLO, ZHI, CORNER = 8, 9, 10, 11, 12
SLOTS = 13
AHEAD = 8
DIRECTIONS = ((-1, 0), (1, 0), (0, -1), (0, 1), (-1, -1), (-1, 1), (1, -1), (1, 1))


def take(values, lanes):
    return jnp.take_along_axis(values, lanes, axis=1, mode="promise_in_bounds")


def full(row):
    return jnp.broadcast_to(row, (SUB, LANES))


def total_of(values):
    return jnp.sum(jnp.sum(values, axis=0, keepdims=True), axis=1, keepdims=True)


def kernel(
    owners, members, r_hbm, cidx_hbm, table_hbm, cells_hbm, inv_ref, amap_hbm, diag_hbm,
    x_out, r_out, p_out,
    r_ref, cidx_ref, table_ref, cells_ref, amap_ref, diag_ref, in_sems,
    mats, halves, rot, key_in, lane_in, key_out, lane_out, moved,
    first_ext, first_cols, first_corner_src, first_corners,
    later_ext, later_cols, later_corner_src, later_corners,
    kap, amaps, w_ext, p_ext, r_cur, q_cur, kt, small,
    row_src, rows,
    mat_sems, send_sems, recv_sems, row_send, row_recv,
):
    count = owners * members
    o = lax.axis_index("coarse")
    m = lax.axis_index("fine")
    me = o * members + m
    groups = cells_ref.shape[0]
    sub = lax.broadcasted_iota(jnp.int32, (SUB, LANES), 0)
    lane = lax.broadcasted_iota(jnp.int32, (SUB, LANES), 1)
    zero = jnp.zeros((SUB, LANES), jnp.float32)

    in_copies = [
        pltpu.make_async_copy(src, dst, in_sems.at[at])
        for at, (src, dst) in enumerate(
            (
                (cells_hbm, cells_ref),
                (r_hbm, r_ref),
                (amap_hbm, amap_ref),
                (cidx_hbm, cidx_ref),
                (table_hbm, table_ref),
                (diag_hbm, diag_ref),
            )
        )
    ]
    for copy in in_copies:
        copy.start()
    def mat_copy(u):
        part = pl.ds(u * SUB, SUB)
        return pltpu.make_async_copy(inv_ref.at[part], mats.at[part], mat_sems.at[u])

    for u in range(groups):
        mat_copy(u).start()

    for slot in range(MAIN, CORNER):
        for f in range(3):
            first_ext[slot, f] = zero
        later_ext[slot, 0] = zero
    for c in range(4):
        first_corners[c] = zero
        later_corners[c] = zero

    barrier = pltpu.get_barrier_semaphore()

    def other(d):
        t = lax.rem(me + d, count)
        return {"coarse": lax.div(t, members), "fine": lax.rem(t, members)}

    def announce(d, carry):
        pl.semaphore_signal(barrier, inc=1, device_id=other(d), device_id_type=MESH)
        return carry

    lax.fori_loop(1, count, announce, 0)

    in_copies[0].wait()

    def keys_of(source):
        row = lax.shift_right_logical(source, 7)
        turn = (jnp.bitwise_and(row, 7) - sub) & 7
        return jnp.bitwise_and(row, ~7) + turn, jnp.bitwise_and(source, 127)

    for g in range(groups):
        key, lanes = keys_of(cells_ref[g])
        key_in[g] = key
        lane_in[g] = lanes

    def load_turns(values):
        for g in range(len(values)):
            for turn in range(SUB):
                rot[g * SUB + turn] = (
                    values[g] if turn == 0 else pltpu.roll(values[g], SUB - turn, 0)
                )

    def permuted(key, lanes):
        parts = [zero, zero]
        for k in range(groups * SUB):
            parts[k % 2] = jnp.where(key == k, take(rot[k], lanes), parts[k % 2])
        return parts[0] + parts[1]

    tall = lax.broadcasted_iota(jnp.int32, (groups * SUB, LANES), 0)
    taller = lax.broadcasted_iota(jnp.int32, (LANES, LANES), 0)
    wide = lax.broadcasted_iota(jnp.int32, (groups * SUB, LANES), 1).astype(jnp.float32)

    def find_one(g, carry):
        block = cells_ref[g]
        for b in range(SUB):
            source = block[b : b + 1, :]
            hit = tall == jnp.broadcast_to(lax.shift_right_logical(source, 7), tall.shape)
            number = (g * SUB + b).astype(jnp.float32)
            left = jnp.concatenate(
                [jnp.where(hit, number, 0.0), jnp.where(hit, wide, 0.0)], axis=0
            ).astype(jnp.bfloat16)
            right = jnp.where(
                taller == jnp.broadcast_to(jnp.bitwise_and(source, 127), taller.shape), 1.0, 0.0
            ).astype(jnp.bfloat16)
            carry = carry + lax.dot_general(
                left, right, (((1,), (1,)), ((), ())), preferred_element_type=jnp.float32
            )
        return carry

    def find(turn, carry):
        return find_one(2 * turn + 1, find_one(2 * turn, carry))

    found = lax.fori_loop(
        0, groups // 2, find, jnp.zeros((2 * groups * SUB, LANES), jnp.float32)
    ).astype(jnp.int32)
    for g in range(groups):
        block = found[g * SUB : (g + 1) * SUB]
        place = found[(groups + g) * SUB : (groups + g + 1) * SUB]
        key, lanes = keys_of(block * LANES + place)
        key_out[g] = key
        lane_out[g] = lanes

    for copy in in_copies[1:]:
        copy.wait()
    small[...] = jnp.zeros(small.shape, jnp.float32)
    small[0, 0:1, 0 : table_ref.shape[1]] = table_ref[...]
    small[1, 0:1, 0 : diag_ref.shape[2]] = diag_ref[0]
    boxes = diag_ref.shape[2]
    table = full(small[0, 0:1, :])
    for x in range(MAIN):
        first_ext[x, 1] = take(table, cidx_ref[x])
        first_ext[x, 2] = (amap_ref[x] + 1).astype(jnp.float32)
        amaps[x] = amap_ref[x]

    def split(values):
        high = values.astype(jnp.bfloat16)
        low = (values - high.astype(jnp.float32)).astype(jnp.bfloat16)
        return high, low

    def block_apply(values, done_with_dot, first=False):
        load_turns(values)

        def some(turn, carry):
            dot, picked = carry
            if first:
                for at in range(AHEAD):
                    mat_copy(turn * AHEAD + at).wait()
            for at in range(AHEAD):
                u = turn * AHEAD + at
                if first:
                    for b in range(SUB):
                        high, low = split(mats[u * SUB + b])
                        halves[u * SUB + b, :, 0:LANES] = high
                        halves[u * SUB + b, :, LANES : 2 * LANES] = low
                ahead = lax.rem(u + 1, groups)
                upcoming = permuted(key_in[ahead], lane_in[ahead])
                left = jnp.concatenate(split(picked), axis=0)
                product = zero
                for b in range(SUB):
                    both = jnp.dot(left, halves[u * SUB + b], preferred_element_type=jnp.float32)
                    line = both[:SUB, :LANES] + (both[SUB:, :LANES] + both[:SUB, LANES:])
                    line = line + both[SUB:, LANES:]
                    product = jnp.where(sub == b, line, product)
                moved[u] = product
                dot = dot + picked * product
                picked = upcoming
            return dot, picked

        dot, _ = lax.fori_loop(
            0, groups // AHEAD, some, (zero, permuted(key_in[0], lane_in[0]))
        )
        done_with_dot(total_of(dot))
        load_turns([moved[g] for g in range(groups)])

        def back(g, carry):
            for step in range(AHEAD):
                at = g * AHEAD + step
                moved[at] = permuted(key_out[at], lane_out[at])
            return carry

        lax.fori_loop(0, groups // AHEAD, back, 0)
        return [moved[g] for g in range(groups)]

    base = lax.shift_right_logical(lane, 3)

    def restrict(values):
        sums = []
        for move in (-1, 0, 1):
            total = zero
            for x in range(MAIN):
                total = total + jnp.where(amaps[x] - base == move, values[x], 0.0)
            sums.append(total)
        total = pltpu.roll(sums[0], LANES - SUB, 1) + sums[1] + pltpu.roll(sums[2], SUB, 1)
        total = full(jnp.sum(total, axis=0, keepdims=True))
        for step in (1, 2, 4):
            total = total + pltpu.roll(total, LANES - step, 1)
        return jnp.where(lane < boxes, restrict_scale * take(total, (lane * SUB) & 127), 0.0)

    def row_copy(index, src, dst, device):
        return pltpu.make_async_remote_copy(
            src_ref=src, dst_ref=dst, send_sem=row_send.at[index], recv_sem=row_recv.at[index],
            device_id=device, device_id_type=MESH,
        )

    def send_rows(index, row):
        row_src[index] = row[0:1, :]
        rows[index, me] = row[0:1, :]

        def one(d, carry):
            row_copy(index, row_src.at[index], rows.at[index, me], other(d)).start()
            return carry

        lax.fori_loop(1, count, one, 0)

    def wait_rows(index):
        part = rows.at[index, pl.ds(0, count - 1)]
        both = row_copy(index, part, part, other(1))
        both.wait_send()
        both.wait_recv()
        return rows[index].reshape(count, LANES)

    def scalar(row, number):
        at = 2 * boxes + number
        return row[:, at : at + 1]

    def with_scalar(row, number, value):
        return jnp.where(lane == 2 * boxes + number, full(value), row)

    def edge_rows(values, z):
        result = zero
        for x in range(MAIN):
            result = jnp.where(sub == x, full(values[x][z : z + 1, :]), result)
        return result

    def halo_copies(ring, ext, cols, corner_src, corners):
        copies = []
        for number, (do, dm) in enumerate(DIRECTIONS):
            if dm == 0:
                src = ext.at[MAIN - 1 if do == 1 else 0]
                dst = ext.at[XLO if do == 1 else XHI]
            elif do == 0:
                src = cols.at[1 if dm == 1 else 0]
                dst = ext.at[ZLO if dm == 1 else ZHI]
            else:
                at = 2 * (0 if do == 1 else 1) + (0 if dm == 1 else 1)
                src = corner_src.at[at]
                dst = corners.at[at]
            to_o, to_m = o + do, m + dm
            from_o, from_m = o - do, m - dm
            goes = (to_o >= 0) & (to_o < owners) & (to_m >= 0) & (to_m < members)
            comes = (from_o >= 0) & (from_o < owners) & (from_m >= 0) & (from_m < members)
            copies.append(
                (
                    goes,
                    comes,
                    pltpu.make_async_remote_copy(
                        src_ref=src, dst_ref=dst,
                        send_sem=send_sems.at[ring, number], recv_sem=recv_sems.at[ring, number],
                        device_id={"coarse": to_o, "fine": to_m}, device_id_type=MESH,
                    ),
                )
            )
        return copies

    def start_halo(ring, fields, ext, cols, corner_src, corners):
        packs = [zero, zero, zero, zero]
        for f, values in enumerate(fields):
            cols[0, f] = edge_rows(values, 0)
            cols[1, f] = edge_rows(values, SUB - 1)
            for side_x in range(2):
                for side_z in range(2):
                    at = 2 * side_x + side_z
                    x = MAIN - 1 if side_x == 0 else 0
                    z = SUB - 1 if side_z == 0 else 0
                    packs[at] = jnp.where(sub == f, full(values[x][z : z + 1, :]), packs[at])
        for at in range(4):
            corner_src[at] = packs[at]
        copies = halo_copies(ring, ext, cols, corner_src, corners)
        for goes, _, copy in copies:
            pl.when(goes)(copy.start)
        return copies

    def wait_halo(copies):
        for goes, comes, copy in copies:
            pl.when(goes)(copy.wait_send)
            pl.when(comes)(copy.wait_recv)

    def corner_rows(corners, f):
        result = zero
        for at in range(4):
            result = jnp.where(sub == at, full(corners[at][f : f + 1, :]), result)
        return result

    def shifted(values, low, high):
        before = jnp.where(sub == 0, full(low), pltpu.roll(values, 1, 0))
        after = jnp.where(sub == SUB - 1, full(high), pltpu.roll(values, SUB - 1, 0))
        return values + 0.5 * (before + after)

    def smear(v):
        planes = [v[XLO]] + [v[x] for x in range(MAIN)] + [v[XHI]]
        corner = v[CORNER]
        low = shifted(v[ZLO], corner[0:1, :], corner[2:3, :])
        high = shifted(v[ZHI], corner[1:2, :], corner[3:4, :])
        result = []
        for x in range(MAIN):
            mid = planes[x + 1] + 0.5 * (planes[x] + planes[x + 2])
            mid = shifted(mid, low[x : x + 1, :], high[x : x + 1, :])
            before = jnp.where(lane == 0, 0.0, pltpu.roll(mid, 1, 1))
            after = jnp.where(lane == LANES - 1, 0.0, pltpu.roll(mid, LANES - 1, 1))
            result.append(mid + 0.5 * (before + after))
        return result

    node = lax.broadcasted_iota(jnp.int32, (count, LANES), 0)
    node_lane = lax.broadcasted_iota(jnp.int32, (count, LANES), 1)
    member = lax.rem(node, members)

    def coarse_solve(source, inverse):
        guess = omega * source * inverse
        for sweep in range(SWEEPS - 1):
            beside = pltpu.roll(guess, 1, 1) + pltpu.roll(guess, LANES - 1, 1)
            beside = beside + jnp.where(member == 0, 0.0, pltpu.roll(guess, 1, 0))
            beside = beside + jnp.where(
                member == members - 1, 0.0, pltpu.roll(guess, count - 1, 0)
            )
            beside = beside + jnp.where(node < members, 0.0, pltpu.roll(guess, members, 0))
            beside = beside + jnp.where(
                node >= count - members, 0.0, pltpu.roll(guess, count - members, 0)
            )
            guess = (1.0 - omega) * guess + omega * (source + beside) * inverse
        return guess

    start = [r_ref[x] for x in range(MAIN)]
    first_row = restrict(start) + pltpu.roll(full(small[1, 0:1, :]), boxes, 1)

    def first_send(dot):
        pl.semaphore_wait(barrier, count - 1)
        send_rows(0, with_scalar(first_row, 0, dot))

    w = block_apply(start, first_send, True)
    for x in range(MAIN):
        first_ext[x, 0] = w[x]
    kappas = [first_ext[x, 1] for x in range(MAIN)]
    maps = [first_ext[x, 2] for x in range(MAIN)]
    copies = start_halo(
        0, [w, kappas, maps], first_ext, first_cols, first_corner_src, first_corners
    )
    gathered = wait_rows(0)
    diagonal = pltpu.roll(gathered, LANES - boxes, 1)
    inverse = jnp.where(
        node_lane < boxes, 1.0 / jnp.where(node_lane < boxes, 6.0 + diagonal, 1.0), 0.0
    )
    source = jnp.where(node_lane < boxes, gathered, 0.0)
    guess = coarse_solve(source, inverse)
    local_part = scalar(jnp.sum(gathered, axis=0, keepdims=True), 0)
    norm = local_part + total_of(source * guess) * (1.0 / restrict_scale)

    def guess_rows(guess):
        picks = {}
        for do in (-1, 0, 1):
            for dm in (-1, 0, 1):
                wanted = me + do * members + dm
                picks[(do, dm)] = full(
                    jnp.sum(jnp.where(node == wanted, guess, 0.0), axis=0, keepdims=True)
                )
        return picks

    def add_coarse(values, guess):
        picks = guess_rows(guess)
        result = []
        for x in range(MAIN):
            result.append(values[x] + take(picks[(0, 0)], amaps[x]))
        for slot, way in ((XLO, (-1, 0)), (XHI, (1, 0)), (ZLO, (0, -1)), (ZHI, (0, 1))):
            result.append(values[slot] + take(picks[way], amaps[slot]))
        corner = zero
        for at, way in enumerate(((-1, -1), (-1, 1), (1, -1), (1, 1))):
            corner = jnp.where(sub == at, take(picks[way], amaps[CORNER]), corner)
        result.append(values[CORNER] + corner)
        return result

    wait_halo(copies)
    for slot in range(SLOTS):
        if slot == CORNER:
            parts = [corner_rows(first_corners, f) for f in range(3)]
        else:
            parts = [first_ext[slot, f] for f in range(3)]
        w_ext[slot] = parts[0]
        kap[slot] = parts[1]
        if slot >= MAIN:
            amaps[slot] = (parts[2].astype(jnp.int32) + (LANES - 1)) & (LANES - 1)
    smeared = smear([kap[s] for s in range(SLOTS)])
    for x in range(MAIN):
        kt[x] = 8.0 * kap[x] + smeared[x]
        r_cur[x] = r_ref[x]
    z = add_coarse([w_ext[s] for s in range(SLOTS)], guess)
    for slot in range(SLOTS):
        p_ext[slot] = z[slot]

    for step in range(ITERS):
        last = step == ITERS - 1
        p = [p_ext[s] for s in range(SLOTS)]
        flat = smear(p)
        steep = smear([p[s] * kap[s] for s in range(SLOTS)])
        along, across = zero, zero
        for x in range(MAIN):
            q = p[x] * kt[x] - kap[x] * flat[x] - steep[x]
            q_cur[x] = q
            along = along + p[x] * q
            across = across + w_ext[x] * q
        image = [q_cur[x] for x in range(MAIN)]
        row = restrict(image)
        row = with_scalar(row, 0, total_of(along))
        row = with_scalar(row, 1, total_of(across))

        def later_send(dot, row=row, step=step):
            send_rows(1 + step, with_scalar(row, 2, dot))

        bq = block_apply(image, later_send)
        if not last:
            for x in range(MAIN):
                later_ext[x, 0] = bq[x]
            copies = start_halo(
                1 + step, [bq], later_ext, later_cols, later_corner_src, later_corners
            )
        gathered = wait_rows(1 + step)
        sums = jnp.sum(gathered, axis=0, keepdims=True)
        alpha = norm / scalar(sums, 0)
        source = source - alpha * jnp.where(node_lane < boxes, gathered, 0.0)
        guess = coarse_solve(source, inverse)
        local_part = (
            local_part - 2.0 * alpha * scalar(sums, 1) + alpha * alpha * scalar(sums, 2)
        )
        following = local_part + total_of(source * guess) * (1.0 / restrict_scale)
        beta = full(following / norm)
        alpha = full(alpha)
        norm = following
        for x in range(MAIN):
            moved_x = alpha * p_ext[x]
            x_out[x] = moved_x if step == 0 else x_out[x] + moved_x
            r_cur[x] = r_cur[x] - alpha * q_cur[x]
        if not last:
            wait_halo(copies)
            change = [later_ext[s, 0] for s in range(CORNER)] + [corner_rows(later_corners, 0)]
            for slot in range(SLOTS):
                w_ext[slot] = w_ext[slot] - alpha * change[slot]
            z = add_coarse([w_ext[s] for s in range(SLOTS)], guess)
            for slot in range(SLOTS):
                p_ext[slot] = z[slot] + beta * p_ext[slot]
        else:
            own = full(jnp.sum(jnp.where(node == me, guess, 0.0), axis=0, keepdims=True))
            for x in range(MAIN):
                z_x = w_ext[x] - alpha * bq[x] + take(own, amaps[x])
                p_out[x] = z_x + beta * p_ext[x]
                r_out[x] = r_cur[x]


def emit(x_ref, r_ref, p_ref, x_out, r_out, p_out, sems):
    pairs = ((x_ref, x_out), (r_ref, r_out), (p_ref, p_out))
    copies = [pltpu.make_async_copy(a, b, sems.at[i]) for i, (a, b) in enumerate(pairs)]
    for copy in copies:
        copy.start()
    for copy in copies:
        copy.wait()


def shards(
    owners, members, right_side, coefficient_index, material_coefficients, block_cells,
    block_inverses, aggregate_map, coarse_diagonal,
):
    blocks, side = block_cells.shape[2], block_cells.shape[3]
    assert right_side.shape == (SUB, SUB, LANES) and side == LANES and blocks == SUB * SUB
    count = owners * members
    groups = blocks // SUB
    field = jax.ShapeDtypeStruct(right_side.shape, jnp.float32)
    vmem = pl.BlockSpec(memory_space=pltpu.VMEM)
    f32, i32 = jnp.float32, jnp.int32
    tile = (SUB, LANES)
    hbm = pl.BlockSpec(memory_space=pltpu.HBM)
    results = pl.pallas_call(
        functools.partial(kernel, owners, members),
        out_shape=(field, field, field),
        in_specs=[hbm] * 7,
        out_specs=(vmem, vmem, vmem),
        scratch_shapes=[
            pltpu.VMEM(right_side.shape, f32),
            pltpu.VMEM(right_side.shape, i32),
            pltpu.VMEM((1,) + material_coefficients.shape, f32),
            pltpu.VMEM((groups,) + tile, i32),
            pltpu.VMEM(right_side.shape, i32),
            pltpu.VMEM(coarse_diagonal.shape, f32),
            pltpu.SemaphoreType.DMA((6,)),
            pltpu.VMEM((blocks, side, side), f32),
            pltpu.VMEM((blocks, side, 2 * side), jnp.bfloat16),
            pltpu.VMEM((blocks,) + tile, f32),
            pltpu.VMEM((groups,) + tile, i32),
            pltpu.VMEM((groups,) + tile, i32),
            pltpu.VMEM((groups,) + tile, i32),
            pltpu.VMEM((groups,) + tile, i32),
            pltpu.VMEM((groups,) + tile, f32),
            pltpu.VMEM((CORNER, 3) + tile, f32),
            pltpu.VMEM((2, 3) + tile, f32),
            pltpu.VMEM((4,) + tile, f32),
            pltpu.VMEM((4,) + tile, f32),
            pltpu.VMEM((CORNER, 1) + tile, f32),
            pltpu.VMEM((2, 1) + tile, f32),
            pltpu.VMEM((4,) + tile, f32),
            pltpu.VMEM((4,) + tile, f32),
            pltpu.VMEM((SLOTS,) + tile, f32),
            pltpu.VMEM((SLOTS,) + tile, i32),
            pltpu.VMEM((SLOTS,) + tile, f32),
            pltpu.VMEM((SLOTS,) + tile, f32),
            pltpu.VMEM((MAIN,) + tile, f32),
            pltpu.VMEM((MAIN,) + tile, f32),
            pltpu.VMEM((MAIN,) + tile, f32),
            pltpu.VMEM((2,) + tile, f32),
            pltpu.VMEM((1 + ITERS, 1, LANES), f32),
            pltpu.VMEM((1 + ITERS, count, 1, LANES), f32),
            pltpu.SemaphoreType.DMA((groups,)),
            pltpu.SemaphoreType.DMA((ITERS, len(DIRECTIONS))),
            pltpu.SemaphoreType.DMA((ITERS, len(DIRECTIONS))),
            pltpu.SemaphoreType.DMA((1 + ITERS,)),
            pltpu.SemaphoreType.DMA((1 + ITERS,)),
        ],
        compiler_params=pltpu.CompilerParams(
            collective_id=0, has_side_effects=True, vmem_limit_bytes=32 << 20
        ),
    )(
        *(pltpu.with_memory_space_constraint(a, pltpu.HBM) for a in (
        right_side,
        coefficient_index,
        material_coefficients.reshape(1, -1),
        block_cells.reshape(groups, SUB, LANES),
        block_inverses.reshape(blocks, side, side),
        aggregate_map,
        coarse_diagonal,
        ))
    )
    return pl.pallas_call(
        emit,
        out_shape=(field, field, field),
        in_specs=[vmem] * 3,
        out_specs=(hbm,) * 3,
        scratch_shapes=[pltpu.SemaphoreType.DMA((3,))],
        compiler_params=pltpu.CompilerParams(vmem_limit_bytes=1 << 20),
    )(*results)


def solution(mesh):
    three = P("coarse", "fine", None)
    return jax.shard_map(
        functools.partial(shards, mesh.shape["coarse"], mesh.shape["fine"]),
        mesh=mesh,
        in_specs=(
            three,
            three,
            P(),
            P("coarse", "fine", None, None),
            P("coarse", "fine", None, None, None),
            three,
            three,
        ),
        out_specs=(three, three, three),
        check_vma=False,
    )
```

profile of v0, /device:TPU:0, one launch (start us, length us, event | category | flops | bytes accessed | tf_op | source)
XLA Modules:
  0.0 28.0 jit_solution(16179340176108874154)
XLA Ops:
  0.6 26.7 %shard_map.94 = (f32[8,8,128]{2,1,0:T(8,128)S(1)}, f32[8,8,128]{2,1,0:T(8,128)S(1)}, f32[8,8,128]{2,1,0:T(8,128)S(1)}) custom-call(f32[8,8,128]{2,1,0:T(8,128)} %r_hbm.1, s32[8,8,128]{2,1,0:T(8,128)} %cidx_hbm.1, f32[1,16]{1,0:T(1,128)} %bitcast.5, s32[8,8,128]{2,1,0:T(8,128)} %bitcast.4, f32[64,128,128]{2,1,0:T(8,128)} %bitcast.3, s32[8,8,128]{2,1,0:T(8,128)} %amap_hbm.1, ...), custom_call_target="tpu_custom_call" | custom-call | tf_op jit(solution)/shard_map/pallas_call | solution.py:512
  27.3 0.7 %shard_map.95 = (f32[8,8,128]{2,1,0:T(8,128)}, f32[8,8,128]{2,1,0:T(8,128)}, f32[8,8,128]{2,1,0:T(8,128)}) custom-call(f32[8,8,128]{2,1,0:T(8,128)S(1)} %get-tuple-element.6.x_ref, f32[8,8,128]{2,1,0:T(8,128)S(1)} %get-tuple-element.7.r_ref, f32[8,8,128]{2,1,0:T(8,128)S(1)} %get-tuple-element.8.p_ref), custom_call_target="tpu_custom_call" | custom-call | tf_op jit(solution)/shard_map/pallas_call | solution.py:571
where the time goes:
time: 28.1 us; the launch traced here: 28 us
  Pallas kernels  27.3 us (97%)
  between operations  0.64 us (2%)
    pallas_call x1, Pallas kernels, shards(): pl.pallas_call(functools.partial(kernel, owners, members), out_shape=(fie...  26.7 us
    pallas_call x1, Pallas kernels, shards(): pl.pallas_call(emit, out_shape=(field, field, field), in_specs=[vmem] * 3...  0.67 us

commit v1 on v0

--- a/solution.py
+++ b/solution.py
@@ -7,7 +7,7 @@
 from jax.experimental.pallas import tpu as pltpu
 from jax.sharding import PartitionSpec as P
 
-ITERS = 2
+ROUNDS = 3
 SWEEPS = 4
 omega = 0.8
 restrict_scale = 0.25
@@ -18,6 +18,7 @@
 XLO, XHI, ZLO, ZHI, CORNER = 8, 9, 10, 11, 12
 SLOTS = 13
 AHEAD = 8
+REACH = SWEEPS
 DIRECTIONS = ((-1, 0), (1, 0), (0, -1), (0, 1), (-1, -1), (-1, 1), (1, -1), (1, 1))
 
 
@@ -39,8 +40,9 @@
     r_ref, cidx_ref, table_ref, cells_ref, amap_ref, diag_ref, in_sems,
     mats, halves, rot, key_in, lane_in, key_out, lane_out, moved,
     first_ext, first_cols, first_corner_src, first_corners,
-    later_ext, later_cols, later_corner_src, later_corners,
-    kap, amaps, w_ext, p_ext, r_cur, q_cur, kt, small,
+    w_ext, w_cols, w_corner_src, w_corners,
+    b_ext, b_cols, b_corner_src, b_corners,
+    kap, amaps, p_ext, u_ext, q_cur, v_cur, kt, small,
     row_src, rows,
     mat_sems, send_sems, recv_sems, row_send, row_recv,
 ):
@@ -76,24 +78,50 @@
         mat_copy(u).start()
 
     for slot in range(MAIN, CORNER):
-        for f in range(3):
+        for f in range(2):
             first_ext[slot, f] = zero
-        later_ext[slot, 0] = zero
+        w_ext[slot, 0] = zero
+        b_ext[slot, 0] = zero
     for c in range(4):
         first_corners[c] = zero
-        later_corners[c] = zero
+        w_corners[c] = zero
+        b_corners[c] = zero
+    rows[...] = jnp.zeros(rows.shape, jnp.float32)
 
     barrier = pltpu.get_barrier_semaphore()
+    reach_o = max(REACH, -(-(owners - 1) // 3))
+    reach_m = max(REACH, -(-(members - 1) // 3))
+    low_o, high_o = jnp.maximum(o - reach_o, 0), jnp.minimum(o + reach_o, owners - 1) + 1
+    low_m, high_m = jnp.maximum(m - reach_m, 0), jnp.minimum(m + reach_m, members - 1) + 1
+    near = (high_o - low_o) * (high_m - low_m) - 1
+
+    def spans(size, reach):
+        return {min(at + reach, size - 1) - max(at - reach, 0) + 1 for at in range(size)}
+
+    near_counts = sorted(
+        {a * b - 1 for a in spans(owners, reach_o) for b in spans(members, reach_m)}
+    )
+
+    def for_near(act):
+        def one_owner(to_o, carry):
+            def one(to_m, inner):
+                @pl.when((to_o != o) | (to_m != m))
+                def _():
+                    act({"coarse": to_o, "fine": to_m})
+
+                return inner
+
+            return lax.fori_loop(low_m, high_m, one, carry)
+
+        lax.fori_loop(low_o, high_o, one_owner, 0)
 
     def other(d):
         t = lax.rem(me + d, count)
         return {"coarse": lax.div(t, members), "fine": lax.rem(t, members)}
 
-    def announce(d, carry):
-        pl.semaphore_signal(barrier, inc=1, device_id=other(d), device_id_type=MESH)
-        return carry
-
-    lax.fori_loop(1, count, announce, 0)
+    for_near(
+        lambda device: pl.semaphore_signal(barrier, inc=1, device_id=device, device_id_type=MESH)
+    )
 
     in_copies[0].wait()
 
@@ -162,8 +190,8 @@
     boxes = diag_ref.shape[2]
     table = full(small[0, 0:1, :])
     for x in range(MAIN):
-        first_ext[x, 1] = take(table, cidx_ref[x])
-        first_ext[x, 2] = (amap_ref[x] + 1).astype(jnp.float32)
+        first_ext[x, 0] = take(table, cidx_ref[x])
+        first_ext[x, 1] = (amap_ref[x] + 1).astype(jnp.float32)
         amaps[x] = amap_ref[x]
 
     def split(values):
@@ -203,7 +231,8 @@
         dot, _ = lax.fori_loop(
             0, groups // AHEAD, some, (zero, permuted(key_in[0], lane_in[0]))
         )
-        done_with_dot(total_of(dot))
+        if done_with_dot is not None:
+            done_with_dot(total_of(dot))
         load_turns([moved[g] for g in range(groups)])
 
         def back(g, carry):
@@ -236,21 +265,35 @@
             device_id=device, device_id_type=MESH,
         )
 
-    def send_rows(index, row):
+    def send_rows(index, row, everywhere=False):
         row_src[index] = row[0:1, :]
         rows[index, me] = row[0:1, :]
-
-        def one(d, carry):
-            row_copy(index, row_src.at[index], rows.at[index, me], other(d)).start()
-            return carry
-
-        lax.fori_loop(1, count, one, 0)
-
-    def wait_rows(index):
-        part = rows.at[index, pl.ds(0, count - 1)]
-        both = row_copy(index, part, part, other(1))
-        both.wait_send()
-        both.wait_recv()
+        if everywhere:
+
+            def one(d, carry):
+                row_copy(index, row_src.at[index], rows.at[index, me], other(d)).start()
+                return carry
+
+            lax.fori_loop(1, count, one, 0)
+        else:
+            for_near(
+                lambda device: row_copy(
+                    index, row_src.at[index], rows.at[index, me], device
+                ).start()
+            )
+
+    def wait_rows(index, everywhere=False):
+        def wait_for(number):
+            part = rows.at[index, pl.ds(0, number)]
+            both = row_copy(index, part, part, other(1))
+            both.wait_send()
+            both.wait_recv()
+
+        if everywhere:
+            wait_for(count - 1)
+        else:
+            for number in near_counts:
+                pl.when(near == number)(functools.partial(wait_for, number))
         return rows[index].reshape(count, LANES)
 
     def scalar(row, number):
@@ -363,30 +406,34 @@
             guess = (1.0 - omega) * guess + omega * (source + beside) * inverse
         return guess
 
+    def only_boxes(values):
+        return jnp.where(node_lane < boxes, values, 0.0)
+
+    def dot_of(left, right):
+        total = zero
+        for x in range(MAIN):
+            total = total + left[x] * right[x]
+        return total_of(total)
+
     start = [r_ref[x] for x in range(MAIN)]
-    first_row = restrict(start) + pltpu.roll(full(small[1, 0:1, :]), boxes, 1)
-
-    def first_send(dot):
-        pl.semaphore_wait(barrier, count - 1)
-        send_rows(0, with_scalar(first_row, 0, dot))
-
-    w = block_apply(start, first_send, True)
+    spread = full(small[1, 0:1, :])
+    spread = jnp.where(lane < boxes, 1.0 / jnp.where(lane < boxes, 6.0 + spread, 1.0), 0.0)
+    spread = pltpu.roll(spread, boxes, 1)
+    first_row = restrict(start) + spread
+    pl.semaphore_wait(barrier, near)
+    send_rows(0, first_row)
+    kappas = [first_ext[x, 0] for x in range(MAIN)]
+    maps = [first_ext[x, 1] for x in range(MAIN)]
+    first_copies = start_halo(
+        0, [kappas, maps], first_ext, first_cols, first_corner_src, first_corners
+    )
+    w = block_apply(start, None, True)
     for x in range(MAIN):
-        first_ext[x, 0] = w[x]
-    kappas = [first_ext[x, 1] for x in range(MAIN)]
-    maps = [first_ext[x, 2] for x in range(MAIN)]
-    copies = start_halo(
-        0, [w, kappas, maps], first_ext, first_cols, first_corner_src, first_corners
-    )
+        w_ext[x, 0] = w[x]
+    w_copies = start_halo(1, [w], w_ext, w_cols, w_corner_src, w_corners)
     gathered = wait_rows(0)
-    diagonal = pltpu.roll(gathered, LANES - boxes, 1)
-    inverse = jnp.where(
-        node_lane < boxes, 1.0 / jnp.where(node_lane < boxes, 6.0 + diagonal, 1.0), 0.0
-    )
-    source = jnp.where(node_lane < boxes, gathered, 0.0)
-    guess = coarse_solve(source, inverse)
-    local_part = scalar(jnp.sum(gathered, axis=0, keepdims=True), 0)
-    norm = local_part + total_of(source * guess) * (1.0 / restrict_scale)
+    inverse = only_boxes(pltpu.roll(gathered, LANES - boxes, 1))
+    guess = coarse_solve(only_boxes(gathered), inverse)
 
     def guess_rows(guess):
         picks = {}
@@ -411,80 +458,84 @@
         result.append(values[CORNER] + corner)
         return result
 
-    wait_halo(copies)
+    wait_halo(first_copies)
     for slot in range(SLOTS):
         if slot == CORNER:
-            parts = [corner_rows(first_corners, f) for f in range(3)]
+            parts = [corner_rows(first_corners, f) for f in range(2)]
         else:
-            parts = [first_ext[slot, f] for f in range(3)]
-        w_ext[slot] = parts[0]
-        kap[slot] = parts[1]
+            parts = [first_ext[slot, f] for f in range(2)]
+        kap[slot] = parts[0]
         if slot >= MAIN:
-            amaps[slot] = (parts[2].astype(jnp.int32) + (LANES - 1)) & (LANES - 1)
+            amaps[slot] = (parts[1].astype(jnp.int32) + (LANES - 1)) & (LANES - 1)
     smeared = smear([kap[s] for s in range(SLOTS)])
     for x in range(MAIN):
         kt[x] = 8.0 * kap[x] + smeared[x]
-        r_cur[x] = r_ref[x]
-    z = add_coarse([w_ext[s] for s in range(SLOTS)], guess)
+
+    def arrived(copies, ext, corners):
+        wait_halo(copies)
+        return [ext[s, 0] for s in range(CORNER)] + [corner_rows(corners, 0)]
+
+    def fine_operate(field, result):
+        flat = smear(field)
+        steep = smear([field[s] * kap[s] for s in range(SLOTS)])
+        for x in range(MAIN):
+            result[x] = field[x] * kt[x] - kap[x] * flat[x] - steep[x]
+
+    z = add_coarse(arrived(w_copies, w_ext, w_corners), guess)
     for slot in range(SLOTS):
         p_ext[slot] = z[slot]
-
-    for step in range(ITERS):
-        last = step == ITERS - 1
-        p = [p_ext[s] for s in range(SLOTS)]
-        flat = smear(p)
-        steep = smear([p[s] * kap[s] for s in range(SLOTS)])
-        along, across = zero, zero
-        for x in range(MAIN):
-            q = p[x] * kt[x] - kap[x] * flat[x] - steep[x]
-            q_cur[x] = q
-            along = along + p[x] * q
-            across = across + w_ext[x] * q
-        image = [q_cur[x] for x in range(MAIN)]
-        row = restrict(image)
-        row = with_scalar(row, 0, total_of(along))
-        row = with_scalar(row, 1, total_of(across))
-
-        def later_send(dot, row=row, step=step):
-            send_rows(1 + step, with_scalar(row, 2, dot))
-
-        bq = block_apply(image, later_send)
-        if not last:
-            for x in range(MAIN):
-                later_ext[x, 0] = bq[x]
-            copies = start_halo(
-                1 + step, [bq], later_ext, later_cols, later_corner_src, later_corners
-            )
-        gathered = wait_rows(1 + step)
-        sums = jnp.sum(gathered, axis=0, keepdims=True)
-        alpha = norm / scalar(sums, 0)
-        source = source - alpha * jnp.where(node_lane < boxes, gathered, 0.0)
-        guess = coarse_solve(source, inverse)
-        local_part = (
-            local_part - 2.0 * alpha * scalar(sums, 1) + alpha * alpha * scalar(sums, 2)
-        )
-        following = local_part + total_of(source * guess) * (1.0 / restrict_scale)
-        beta = full(following / norm)
-        alpha = full(alpha)
-        norm = following
-        for x in range(MAIN):
-            moved_x = alpha * p_ext[x]
-            x_out[x] = moved_x if step == 0 else x_out[x] + moved_x
-            r_cur[x] = r_cur[x] - alpha * q_cur[x]
-        if not last:
-            wait_halo(copies)
-            change = [later_ext[s, 0] for s in range(CORNER)] + [corner_rows(later_corners, 0)]
-            for slot in range(SLOTS):
-                w_ext[slot] = w_ext[slot] - alpha * change[slot]
-            z = add_coarse([w_ext[s] for s in range(SLOTS)], guess)
-            for slot in range(SLOTS):
-                p_ext[slot] = z[slot] + beta * p_ext[slot]
-        else:
-            own = full(jnp.sum(jnp.where(node == me, guess, 0.0), axis=0, keepdims=True))
-            for x in range(MAIN):
-                z_x = w_ext[x] - alpha * bq[x] + take(own, amaps[x])
-                p_out[x] = z_x + beta * p_ext[x]
-                r_out[x] = r_cur[x]
+    fine_operate(z, q_cur)
+    image = [q_cur[x] for x in range(MAIN)]
+    send_rows(1, restrict(image))
+    bq = block_apply(image, None)
+    for x in range(MAIN):
+        b_ext[x, 0] = bq[x]
+    b_copies = start_halo(2, [bq], b_ext, b_cols, b_corner_src, b_corners)
+    r_dot_p = dot_of(r_ref, p_ext)
+    p_dot_q = dot_of(p_ext, q_cur)
+    guess = coarse_solve(only_boxes(wait_rows(1)), inverse)
+    u = add_coarse(arrived(b_copies, b_ext, b_corners), guess)
+    for x in range(MAIN):
+        u_ext[x] = u[x]
+    fine_operate(u, v_cur)
+    image = [v_cur[x] for x in range(MAIN)]
+    row = restrict(image) + spread
+    row = with_scalar(row, 0, r_dot_p)
+    row = with_scalar(row, 1, p_dot_q)
+    row = with_scalar(row, 2, dot_of(q_cur, u_ext))
+    row = with_scalar(row, 3, dot_of(u_ext, v_cur))
+
+    def last_send(dot):
+        send_rows(2, with_scalar(row, 4, dot), True)
+
+    bv = block_apply(image, last_send)
+    gathered = wait_rows(2, True)
+    sums = jnp.sum(gathered, axis=0, keepdims=True)
+    inverse = only_boxes(pltpu.roll(gathered, LANES - boxes, 1))
+    source = only_boxes(gathered)
+    guess = coarse_solve(source, inverse)
+    mu = [scalar(sums, number) for number in range(5)]
+    mu[4] = mu[4] + total_of(source * guess) * (1.0 / restrict_scale)
+    alpha0 = mu[0] / mu[1]
+    norm1 = mu[0] - 2.0 * alpha0 * mu[1] + alpha0 * alpha0 * mu[2]
+    grow = 1.0 + norm1 / mu[0]
+    curve = grow * grow * mu[1] - 2.0 * grow * alpha0 * mu[2] + alpha0 * alpha0 * mu[3]
+    alpha1 = norm1 / curve
+    cross = grow * mu[1] - (1.0 + grow) * alpha0 * mu[2] + alpha0 * alpha0 * mu[3]
+    square = grow * grow * mu[2] - 2.0 * grow * alpha0 * mu[3] + alpha0 * alpha0 * mu[4]
+    norm2 = norm1 - 2.0 * alpha1 * cross + alpha1 * alpha1 * square
+    beta1 = full(norm2 / norm1)
+    alpha0, alpha1, grow = full(alpha0), full(alpha1), full(grow)
+    own = full(jnp.sum(jnp.where(node == me, guess, 0.0), axis=0, keepdims=True))
+    for x in range(MAIN):
+        p0, q0, u0, v0 = p_ext[x], q_cur[x], u_ext[x], v_cur[x]
+        t0 = bv[x] + take(own, amaps[x])
+        p1 = grow * p0 - alpha0 * u0
+        q1 = grow * q0 - alpha0 * v0
+        x_out[x] = alpha0 * p0 + alpha1 * p1
+        r_out[x] = r_ref[x] - alpha0 * q0 - alpha1 * q1
+        z2 = p0 - alpha0 * u0 - alpha1 * (grow * u0 - alpha0 * t0)
+        p_out[x] = z2 + beta1 * p1
 
 
 def emit(x_ref, r_ref, p_ref, x_out, r_out, p_out, sems):
@@ -530,8 +581,12 @@
             pltpu.VMEM((groups,) + tile, i32),
             pltpu.VMEM((groups,) + tile, i32),
             pltpu.VMEM((groups,) + tile, f32),
-            pltpu.VMEM((CORNER, 3) + tile, f32),
-            pltpu.VMEM((2, 3) + tile, f32),
+            pltpu.VMEM((CORNER, 2) + tile, f32),
+            pltpu.VMEM((2, 2) + tile, f32),
+            pltpu.VMEM((4,) + tile, f32),
+            pltpu.VMEM((4,) + tile, f32),
+            pltpu.VMEM((CORNER, 1) + tile, f32),
+            pltpu.VMEM((2, 1) + tile, f32),
             pltpu.VMEM((4,) + tile, f32),
             pltpu.VMEM((4,) + tile, f32),
             pltpu.VMEM((CORNER, 1) + tile, f32),
@@ -541,18 +596,18 @@
             pltpu.VMEM((SLOTS,) + tile, f32),
             pltpu.VMEM((SLOTS,) + tile, i32),
             pltpu.VMEM((SLOTS,) + tile, f32),
-            pltpu.VMEM((SLOTS,) + tile, f32),
+            pltpu.VMEM((MAIN,) + tile, f32),
             pltpu.VMEM((MAIN,) + tile, f32),
             pltpu.VMEM((MAIN,) + tile, f32),
             pltpu.VMEM((MAIN,) + tile, f32),
             pltpu.VMEM((2,) + tile, f32),
-            pltpu.VMEM((1 + ITERS, 1, LANES), f32),
-            pltpu.VMEM((1 + ITERS, count, 1, LANES), f32),
+            pltpu.VMEM((ROUNDS, 1, LANES), f32),
+            pltpu.VMEM((ROUNDS, count, 1, LANES), f32),
             pltpu.SemaphoreType.DMA((groups,)),
-            pltpu.SemaphoreType.DMA((ITERS, len(DIRECTIONS))),
-            pltpu.SemaphoreType.DMA((ITERS, len(DIRECTIONS))),
-            pltpu.SemaphoreType.DMA((1 + ITERS,)),
-            pltpu.SemaphoreType.DMA((1 + ITERS,)),
+            pltpu.SemaphoreType.DMA((ROUNDS, len(DIRECTIONS))),
+            pltpu.SemaphoreType.DMA((ROUNDS, len(DIRECTIONS))),
+            pltpu.SemaphoreType.DMA((ROUNDS,)),
+            pltpu.SemaphoreType.DMA((ROUNDS,)),
         ],
         compiler_params=pltpu.CompilerParams(
             collective_id=0, has_side_effects=True, vmem_limit_bytes=32 << 20

time: 28.1 us -> 25.4 us (0.904)
  Pallas kernels: 27.3 us -> 24.6 us
    pallas_call x1, Pallas kernels: 26.7 us -> 24 us  [shards(): pl.pallas_call(functools.partial(kernel, owners, members), out_shape=(fie...]
where the time goes in v1:
time: 25.4 us; the launch traced here: 25.3 us
  Pallas kernels  24.6 us (97%)
  between operations  0.64 us (3%)
    pallas_call x1, Pallas kernels, shards(): pl.pallas_call(functools.partial(kernel, owners, members), out_shape=(fie...  24 us
    pallas_call x1, Pallas kernels, shards(): pl.pallas_call(emit, out_shape=(field, field, field), in_specs=[vmem] * 3...  0.67 us

profile of v1, /device:TPU:0, one launch (start us, length us, event | category | flops | bytes accessed | tf_op | source)
XLA Modules:
  0.0 25.3 jit_solution(13039256793546869828)
XLA Ops:
  0.6 24.0 %shard_map.94 = (f32[8,8,128]{2,1,0:T(8,128)S(1)}, f32[8,8,128]{2,1,0:T(8,128)S(1)}, f32[8,8,128]{2,1,0:T(8,128)S(1)}) custom-call(f32[8,8,128]{2,1,0:T(8,128)} %r_hbm.1, s32[8,8,128]{2,1,0:T(8,128)} %cidx_hbm.1, f32[1,16]{1,0:T(1,128)} %bitcast.5, s32[8,8,128]{2,1,0:T(8,128)} %bitcast.4, f32[64,128,128]{2,1,0:T(8,128)} %bitcast.3, s32[8,8,128]{2,1,0:T(8,128)} %amap_hbm.1, ...), custom_call_target="tpu_custom_call" | custom-call | tf_op jit(solution)/shard_map/pallas_call | solution.py:563
  24.6 0.7 %shard_map.95 = (f32[8,8,128]{2,1,0:T(8,128)}, f32[8,8,128]{2,1,0:T(8,128)}, f32[8,8,128]{2,1,0:T(8,128)}) custom-call(f32[8,8,128]{2,1,0:T(8,128)S(1)} %get-tuple-element.6.x_ref, f32[8,8,128]{2,1,0:T(8,128)S(1)} %get-tuple-element.7.r_ref, f32[8,8,128]{2,1,0:T(8,128)S(1)} %get-tuple-element.8.p_ref), custom_call_target="tpu_custom_call" | custom-call | tf_op jit(solution)/shard_map/pallas_call | solution.py:626

commit v2 on v1

--- a/solution.py
+++ b/solution.py
@@ -7,7 +7,9 @@
 from jax.experimental.pallas import tpu as pltpu
 from jax.sharding import PartitionSpec as P
 
-ROUNDS = 3
+RINGS = 3
+ROUNDS = 4
+UNROLLED = 64
 SWEEPS = 4
 omega = 0.8
 restrict_scale = 0.25
@@ -17,7 +19,6 @@
 MAIN = 8
 XLO, XHI, ZLO, ZHI, CORNER = 8, 9, 10, 11, 12
 SLOTS = 13
-AHEAD = 8
 REACH = SWEEPS
 DIRECTIONS = ((-1, 0), (1, 0), (0, -1), (0, 1), (-1, -1), (-1, 1), (1, -1), (1, 1))
 
@@ -43,7 +44,7 @@
     w_ext, w_cols, w_corner_src, w_corners,
     b_ext, b_cols, b_corner_src, b_corners,
     kap, amaps, p_ext, u_ext, q_cur, v_cur, kt, small,
-    row_src, rows,
+    row_src, rows, picks,
     mat_sems, send_sems, recv_sems, row_send, row_recv,
 ):
     count = owners * members
@@ -74,9 +75,6 @@
         part = pl.ds(u * SUB, SUB)
         return pltpu.make_async_copy(inv_ref.at[part], mats.at[part], mat_sems.at[u])
 
-    for u in range(groups):
-        mat_copy(u).start()
-
     for slot in range(MAIN, CORNER):
         for f in range(2):
             first_ext[slot, f] = zero
@@ -102,28 +100,46 @@
         {a * b - 1 for a in spans(owners, reach_o) for b in spans(members, reach_m)}
     )
 
-    def for_near(act):
-        def one_owner(to_o, carry):
-            def one(to_m, inner):
-                @pl.when((to_o != o) | (to_m != m))
-                def _():
-                    act({"coarse": to_o, "fine": to_m})
-
-                return inner
-
-            return lax.fori_loop(low_m, high_m, one, carry)
-
-        lax.fori_loop(low_o, high_o, one_owner, 0)
-
     def other(d):
         t = lax.rem(me + d, count)
         return {"coarse": lax.div(t, members), "fine": lax.rem(t, members)}
 
+    def for_all(act):
+        if count <= UNROLLED:
+            for d in range(1, count):
+                act(other(d))
+        else:
+
+            def one(d, carry):
+                act(other(d))
+                return carry
+
+            lax.fori_loop(1, count, one, 0)
+
+    def for_near(act):
+        def one(device):
+            to_o, to_m = device["coarse"], device["fine"]
+            close = None
+            if reach_o < owners - 1:
+                close = (to_o >= low_o) & (to_o < high_o)
+            if reach_m < members - 1:
+                close_m = (to_m >= low_m) & (to_m < high_m)
+                close = close_m if close is None else close & close_m
+            if close is None:
+                act(device)
+            else:
+                pl.when(close)(functools.partial(act, device))
+
+        for_all(one)
+
     for_near(
         lambda device: pl.semaphore_signal(barrier, inc=1, device_id=device, device_id_type=MESH)
     )
 
-    in_copies[0].wait()
+    for u in range(groups):
+        mat_copy(u).start()
+    for copy in in_copies:
+        copy.wait()
 
     def keys_of(source):
         row = lax.shift_right_logical(source, 7)
@@ -148,42 +164,41 @@
             parts[k % 2] = jnp.where(key == k, take(rot[k], lanes), parts[k % 2])
         return parts[0] + parts[1]
 
-    tall = lax.broadcasted_iota(jnp.int32, (groups * SUB, LANES), 0)
-    taller = lax.broadcasted_iota(jnp.int32, (LANES, LANES), 0)
-    wide = lax.broadcasted_iota(jnp.int32, (groups * SUB, LANES), 1).astype(jnp.float32)
-
-    def find_one(g, carry):
+    both_lanes = 2 * LANES
+    tall = lax.broadcasted_iota(jnp.int32, (groups * SUB, both_lanes), 0)
+    taller = lax.broadcasted_iota(jnp.int32, (LANES, both_lanes), 0)
+    place = lax.broadcasted_iota(jnp.int32, (groups * SUB, both_lanes), 1)
+    second = jnp.where(place >= LANES, 1.0, 0.0)
+
+    def narrow(values):
+        return values.astype(jnp.float32).astype(jnp.bfloat16)
+
+    tall, taller, place = narrow(tall), narrow(taller), narrow(place & (LANES - 1))
+    one, nothing = jnp.bfloat16(1), jnp.bfloat16(0)
+    found = jnp.zeros((2 * groups * SUB, LANES), jnp.float32)
+    for g in range(groups):
         block = cells_ref[g]
-        for b in range(SUB):
-            source = block[b : b + 1, :]
-            hit = tall == jnp.broadcast_to(lax.shift_right_logical(source, 7), tall.shape)
-            number = (g * SUB + b).astype(jnp.float32)
+        for b in range(0, SUB, 2):
+            source = jnp.concatenate([block[b : b + 1, :], block[b + 1 : b + 2, :]], axis=1)
+            row = narrow(lax.shift_right_logical(source, 7))
+            hit = tall == jnp.broadcast_to(row, tall.shape)
+            number = (second + (g * SUB + b)).astype(jnp.bfloat16)
             left = jnp.concatenate(
-                [jnp.where(hit, number, 0.0), jnp.where(hit, wide, 0.0)], axis=0
-            ).astype(jnp.bfloat16)
-            right = jnp.where(
-                taller == jnp.broadcast_to(jnp.bitwise_and(source, 127), taller.shape), 1.0, 0.0
-            ).astype(jnp.bfloat16)
-            carry = carry + lax.dot_general(
+                [jnp.where(hit, number, nothing), jnp.where(hit, place, nothing)], axis=0
+            )
+            column = narrow(jnp.bitwise_and(source, LANES - 1))
+            right = jnp.where(taller == jnp.broadcast_to(column, taller.shape), one, nothing)
+            found = found + lax.dot_general(
                 left, right, (((1,), (1,)), ((), ())), preferred_element_type=jnp.float32
             )
-        return carry
-
-    def find(turn, carry):
-        return find_one(2 * turn + 1, find_one(2 * turn, carry))
-
-    found = lax.fori_loop(
-        0, groups // 2, find, jnp.zeros((2 * groups * SUB, LANES), jnp.float32)
-    ).astype(jnp.int32)
+    found = found.astype(jnp.int32)
     for g in range(groups):
         block = found[g * SUB : (g + 1) * SUB]
-        place = found[(groups + g) * SUB : (groups + g + 1) * SUB]
-        key, lanes = keys_of(block * LANES + place)
+        spot = found[(groups + g) * SUB : (groups + g + 1) * SUB]
+        key, lanes = keys_of(block * LANES + spot)
         key_out[g] = key
         lane_out[g] = lanes
 
-    for copy in in_copies[1:]:
-        copy.wait()
     small[...] = jnp.zeros(small.shape, jnp.float32)
     small[0, 0:1, 0 : table_ref.shape[1]] = table_ref[...]
     small[1, 0:1, 0 : diag_ref.shape[2]] = diag_ref[0]
@@ -199,50 +214,52 @@
         low = (values - high.astype(jnp.float32)).astype(jnp.bfloat16)
         return high, low
 
-    def block_apply(values, done_with_dot, first=False):
+    odd = (sub & 1) == 1
+
+    def pick(values, keep):
         load_turns(values)
-
-        def some(turn, carry):
-            dot, picked = carry
+        for g in range(groups):
+            keep[g] = permuted(key_in[g], lane_in[g])
+
+    def block_apply(picked_of, done_with_dot, first=False):
+        dot = zero
+        picked = picked_of(0)
+        for u in range(groups):
             if first:
-                for at in range(AHEAD):
-                    mat_copy(turn * AHEAD + at).wait()
-            for at in range(AHEAD):
-                u = turn * AHEAD + at
-                if first:
-                    for b in range(SUB):
-                        high, low = split(mats[u * SUB + b])
-                        halves[u * SUB + b, :, 0:LANES] = high
-                        halves[u * SUB + b, :, LANES : 2 * LANES] = low
-                ahead = lax.rem(u + 1, groups)
-                upcoming = permuted(key_in[ahead], lane_in[ahead])
-                left = jnp.concatenate(split(picked), axis=0)
-                product = zero
+                mat_copy(u).wait()
                 for b in range(SUB):
-                    both = jnp.dot(left, halves[u * SUB + b], preferred_element_type=jnp.float32)
-                    line = both[:SUB, :LANES] + (both[SUB:, :LANES] + both[:SUB, LANES:])
-                    line = line + both[SUB:, LANES:]
-                    product = jnp.where(sub == b, line, product)
-                moved[u] = product
+                    high, low = split(mats[u * SUB + b])
+                    pair, part = (u * SUB + b) // 2, pl.ds((b % 2) * LANES, LANES)
+                    halves[pair, part, 0:LANES] = high
+                    halves[pair, part, LANES : 2 * LANES] = low
+            upcoming = picked_of(u + 1) if u + 1 < groups else None
+            sides = []
+            for keep_odd in (False, True):
+                side = jnp.where(odd == keep_odd, picked, 0.0)
+                sides.append(jnp.concatenate(split(side), axis=0))
+            left = jnp.concatenate(sides, axis=1)
+            product = zero
+            for j in range(SUB // 2):
+                both = jnp.dot(
+                    left, halves[u * SUB // 2 + j], preferred_element_type=jnp.float32
+                )
+                line = both[:SUB, :LANES] + (both[SUB:, :LANES] + both[:SUB, LANES:])
+                line = line + both[SUB:, LANES:]
+                product = jnp.where(lax.shift_right_logical(sub, 1) == j, line, product)
+            moved[u] = product
+            if done_with_dot is not None:
                 dot = dot + picked * product
-                picked = upcoming
-            return dot, picked
-
-        dot, _ = lax.fori_loop(
-            0, groups // AHEAD, some, (zero, permuted(key_in[0], lane_in[0]))
-        )
+            picked = upcoming
         if done_with_dot is not None:
             done_with_dot(total_of(dot))
         load_turns([moved[g] for g in range(groups)])
-
-        def back(g, carry):
-            for step in range(AHEAD):
-                at = g * AHEAD + step
-                moved[at] = permuted(key_out[at], lane_out[at])
-            return carry
-
-        lax.fori_loop(0, groups // AHEAD, back, 0)
+        for g in range(groups):
+            moved[g] = permuted(key_out[g], lane_out[g])
         return [moved[g] for g in range(groups)]
+
+    def solve(values, done_with_dot=None):
+        load_turns(values)
+        return block_apply(lambda g: permuted(key_in[g], lane_in[g]), done_with_dot)
 
     base = lax.shift_right_logical(lane, 3)
 
@@ -268,19 +285,9 @@
     def send_rows(index, row, everywhere=False):
         row_src[index] = row[0:1, :]
         rows[index, me] = row[0:1, :]
-        if everywhere:
-
-            def one(d, carry):
-                row_copy(index, row_src.at[index], rows.at[index, me], other(d)).start()
-                return carry
-
-            lax.fori_loop(1, count, one, 0)
-        else:
-            for_near(
-                lambda device: row_copy(
-                    index, row_src.at[index], rows.at[index, me], device
-                ).start()
-            )
+        (for_all if everywhere else for_near)(
+            lambda device: row_copy(index, row_src.at[index], rows.at[index, me], device).start()
+        )
 
     def wait_rows(index, everywhere=False):
         def wait_for(number):
@@ -311,7 +318,7 @@
 
     def halo_copies(ring, ext, cols, corner_src, corners):
         copies = []
-        for number, (do, dm) in enumerate(DIRECTIONS):
+        for do, dm in DIRECTIONS:
             if dm == 0:
                 src = ext.at[MAIN - 1 if do == 1 else 0]
                 dst = ext.at[XLO if do == 1 else XHI]
@@ -323,16 +330,13 @@
                 src = corner_src.at[at]
                 dst = corners.at[at]
             to_o, to_m = o + do, m + dm
-            from_o, from_m = o - do, m - dm
             goes = (to_o >= 0) & (to_o < owners) & (to_m >= 0) & (to_m < members)
-            comes = (from_o >= 0) & (from_o < owners) & (from_m >= 0) & (from_m < members)
             copies.append(
                 (
                     goes,
-                    comes,
                     pltpu.make_async_remote_copy(
                         src_ref=src, dst_ref=dst,
-                        send_sem=send_sems.at[ring, number], recv_sem=recv_sems.at[ring, number],
+                        send_sem=send_sems.at[ring], recv_sem=recv_sems.at[ring],
                         device_id={"coarse": to_o, "fine": to_m}, device_id_type=MESH,
                     ),
                 )
@@ -353,14 +357,29 @@
         for at in range(4):
             corner_src[at] = packs[at]
         copies = halo_copies(ring, ext, cols, corner_src, corners)
-        for goes, _, copy in copies:
+        for goes, copy in copies:
             pl.when(goes)(copy.start)
-        return copies
-
-    def wait_halo(copies):
-        for goes, comes, copy in copies:
-            pl.when(goes)(copy.wait_send)
-            pl.when(comes)(copy.wait_recv)
+
+    beside_o = (o > 0).astype(jnp.int32) + (o < owners - 1).astype(jnp.int32)
+    beside_m = (m > 0).astype(jnp.int32) + (m < members - 1).astype(jnp.int32)
+
+    def wait_halo(ring, fields):
+        for number_o in range(3):
+            for number_m in range(3):
+                tiles = fields * (number_o + number_m) + number_o * number_m
+                if tiles == 0:
+                    continue
+
+                @pl.when((beside_o == number_o) & (beside_m == number_m))
+                def _(tiles=tiles):
+                    part = rot.at[pl.ds(0, tiles)]
+                    both = pltpu.make_async_remote_copy(
+                        src_ref=part, dst_ref=part,
+                        send_sem=send_sems.at[ring], recv_sem=recv_sems.at[ring],
+                        device_id=other(1), device_id_type=MESH,
+                    )
+                    both.wait_send()
+                    both.wait_recv()
 
     def corner_rows(corners, f):
         result = zero
@@ -420,17 +439,18 @@
     spread = jnp.where(lane < boxes, 1.0 / jnp.where(lane < boxes, 6.0 + spread, 1.0), 0.0)
     spread = pltpu.roll(spread, boxes, 1)
     first_row = restrict(start) + spread
+    pick(start, picks)
     pl.semaphore_wait(barrier, near)
     send_rows(0, first_row)
     kappas = [first_ext[x, 0] for x in range(MAIN)]
     maps = [first_ext[x, 1] for x in range(MAIN)]
-    first_copies = start_halo(
+    start_halo(
         0, [kappas, maps], first_ext, first_cols, first_corner_src, first_corners
     )
-    w = block_apply(start, None, True)
+    w = block_apply(lambda g: picks[g], None, True)
     for x in range(MAIN):
         w_ext[x, 0] = w[x]
-    w_copies = start_halo(1, [w], w_ext, w_cols, w_corner_src, w_corners)
+    start_halo(1, [w], w_ext, w_cols, w_corner_src, w_corners)
     gathered = wait_rows(0)
     inverse = only_boxes(pltpu.roll(gathered, LANES - boxes, 1))
     guess = coarse_solve(only_boxes(gathered), inverse)
@@ -458,7 +478,7 @@
         result.append(values[CORNER] + corner)
         return result
 
-    wait_halo(first_copies)
+    wait_halo(0, 2)
     for slot in range(SLOTS):
         if slot == CORNER:
             parts = [corner_rows(first_corners, f) for f in range(2)]
@@ -471,8 +491,8 @@
     for x in range(MAIN):
         kt[x] = 8.0 * kap[x] + smeared[x]
 
-    def arrived(copies, ext, corners):
-        wait_halo(copies)
+    def arrived(ring, ext, corners):
+        wait_halo(ring, 1)
         return [ext[s, 0] for s in range(CORNER)] + [corner_rows(corners, 0)]
 
     def fine_operate(field, result):
@@ -481,20 +501,20 @@
         for x in range(MAIN):
             result[x] = field[x] * kt[x] - kap[x] * flat[x] - steep[x]
 
-    z = add_coarse(arrived(w_copies, w_ext, w_corners), guess)
+    z = add_coarse(arrived(1, w_ext, w_corners), guess)
     for slot in range(SLOTS):
         p_ext[slot] = z[slot]
     fine_operate(z, q_cur)
     image = [q_cur[x] for x in range(MAIN)]
     send_rows(1, restrict(image))
-    bq = block_apply(image, None)
+    bq = solve(image)
     for x in range(MAIN):
         b_ext[x, 0] = bq[x]
-    b_copies = start_halo(2, [bq], b_ext, b_cols, b_corner_src, b_corners)
+    start_halo(2, [bq], b_ext, b_cols, b_corner_src, b_corners)
     r_dot_p = dot_of(r_ref, p_ext)
     p_dot_q = dot_of(p_ext, q_cur)
     guess = coarse_solve(only_boxes(wait_rows(1)), inverse)
-    u = add_coarse(arrived(b_copies, b_ext, b_corners), guess)
+    u = add_coarse(arrived(2, b_ext, b_corners), guess)
     for x in range(MAIN):
         u_ext[x] = u[x]
     fine_operate(u, v_cur)
@@ -504,29 +524,24 @@
     row = with_scalar(row, 1, p_dot_q)
     row = with_scalar(row, 2, dot_of(q_cur, u_ext))
     row = with_scalar(row, 3, dot_of(u_ext, v_cur))
-
-    def last_send(dot):
-        send_rows(2, with_scalar(row, 4, dot), True)
-
-    bv = block_apply(image, last_send)
+    send_rows(2, row, True)
+    bv = solve(image, lambda dot: send_rows(3, full(dot), True))
     gathered = wait_rows(2, True)
     sums = jnp.sum(gathered, axis=0, keepdims=True)
     inverse = only_boxes(pltpu.roll(gathered, LANES - boxes, 1))
     source = only_boxes(gathered)
     guess = coarse_solve(source, inverse)
-    mu = [scalar(sums, number) for number in range(5)]
-    mu[4] = mu[4] + total_of(source * guess) * (1.0 / restrict_scale)
-    alpha0 = mu[0] / mu[1]
-    norm1 = mu[0] - 2.0 * alpha0 * mu[1] + alpha0 * alpha0 * mu[2]
-    grow = 1.0 + norm1 / mu[0]
-    curve = grow * grow * mu[1] - 2.0 * grow * alpha0 * mu[2] + alpha0 * alpha0 * mu[3]
-    alpha1 = norm1 / curve
-    cross = grow * mu[1] - (1.0 + grow) * alpha0 * mu[2] + alpha0 * alpha0 * mu[3]
-    square = grow * grow * mu[2] - 2.0 * grow * alpha0 * mu[3] + alpha0 * alpha0 * mu[4]
-    norm2 = norm1 - 2.0 * alpha1 * cross + alpha1 * alpha1 * square
-    beta1 = full(norm2 / norm1)
-    alpha0, alpha1, grow = full(alpha0), full(alpha1), full(grow)
+    coarse_part = full(total_of(source * guess) * (1.0 / restrict_scale))
+    mu = [full(scalar(sums, number)) for number in range(4)]
+    turn = 1.0 / mu[1]
+    alpha0 = mu[0] * turn
+    grow = alpha0 * mu[2] * turn
+    curve = 1.0 / (alpha0 * alpha0 * mu[3] - grow * grow * mu[1])
+    alpha1 = mu[0] * (grow - 1.0) * curve
+    part = grow * grow * mu[2] - 2.0 * grow * alpha0 * mu[3] + alpha0 * alpha0 * coarse_part
+    scale = alpha1 * curve
     own = full(jnp.sum(jnp.where(node == me, guess, 0.0), axis=0, keepdims=True))
+    ahead, onward = [], []
     for x in range(MAIN):
         p0, q0, u0, v0 = p_ext[x], q_cur[x], u_ext[x], v_cur[x]
         t0 = bv[x] + take(own, amaps[x])
@@ -534,8 +549,12 @@
         q1 = grow * q0 - alpha0 * v0
         x_out[x] = alpha0 * p0 + alpha1 * p1
         r_out[x] = r_ref[x] - alpha0 * q0 - alpha1 * q1
-        z2 = p0 - alpha0 * u0 - alpha1 * (grow * u0 - alpha0 * t0)
-        p_out[x] = z2 + beta1 * p1
+        ahead.append(p0 - alpha0 * u0 - alpha1 * (grow * u0 - alpha0 * t0))
+        onward.append(p1)
+    last = full(jnp.sum(wait_rows(3, True), axis=0, keepdims=True))
+    beta1 = scale * (part + alpha0 * alpha0 * last) - 1.0
+    for x in range(MAIN):
+        p_out[x] = ahead[x] + beta1 * onward[x]
 
 
 def emit(x_ref, r_ref, p_ref, x_out, r_out, p_out, sems):
@@ -574,7 +593,7 @@
             pltpu.VMEM(coarse_diagonal.shape, f32),
             pltpu.SemaphoreType.DMA((6,)),
             pltpu.VMEM((blocks, side, side), f32),
-            pltpu.VMEM((blocks, side, 2 * side), jnp.bfloat16),
+            pltpu.VMEM((blocks // 2, 2 * side, 2 * side), jnp.bfloat16),
             pltpu.VMEM((blocks,) + tile, f32),
             pltpu.VMEM((groups,) + tile, i32),
             pltpu.VMEM((groups,) + tile, i32),
@@ -603,9 +622,10 @@
             pltpu.VMEM((2,) + tile, f32),
             pltpu.VMEM((ROUNDS, 1, LANES), f32),
             pltpu.VMEM((ROUNDS, count, 1, LANES), f32),
+            pltpu.VMEM((groups,) + tile, f32),
             pltpu.SemaphoreType.DMA((groups,)),
-            pltpu.SemaphoreType.DMA((ROUNDS, len(DIRECTIONS))),
-            pltpu.SemaphoreType.DMA((ROUNDS, len(DIRECTIONS))),
+            pltpu.SemaphoreType.DMA((RINGS,)),
+            pltpu.SemaphoreType.DMA((RINGS,)),
             pltpu.SemaphoreType.DMA((ROUNDS,)),
             pltpu.SemaphoreType.DMA((ROUNDS,)),
         ],

time: 25.4 us -> 24.1 us (0.949)
  Pallas kernels: 24.6 us -> 23.3 us
    pallas_call x1, Pallas kernels: 24 us -> 22.7 us  [shards(): pl.pallas_call(functools.partial(kernel, owners, members), out_shape=(fie...]
where the time goes in v2:
time: 24.1 us; the launch traced here: 24 us
  Pallas kernels  23.3 us (97%)
  between operations  0.64 us (3%)
    pallas_call x1, Pallas kernels, shards(): pl.pallas_call(functools.partial(kernel, owners, members), out_shape=(fie...  22.7 us
    pallas_call x1, Pallas kernels, shards(): pl.pallas_call(emit, out_shape=(field, field, field), in_specs=[vmem] * 3...  0.67 us

profile of v2, /device:TPU:0, one launch (start us, length us, event | category | flops | bytes accessed | tf_op | source)
XLA Modules:
  0.0 24.0 jit_solution(8988456218931768405)
XLA Ops:
  0.6 22.7 %shard_map.94 = (f32[8,8,128]{2,1,0:T(8,128)S(1)}, f32[8,8,128]{2,1,0:T(8,128)S(1)}, f32[8,8,128]{2,1,0:T(8,128)S(1)}) custom-call(f32[8,8,128]{2,1,0:T(8,128)} %r_hbm.1, s32[8,8,128]{2,1,0:T(8,128)} %cidx_hbm.1, f32[1,16]{1,0:T(1,128)} %bitcast.5, s32[8,8,128]{2,1,0:T(8,128)} %bitcast.4, f32[64,128,128]{2,1,0:T(8,128)} %bitcast.3, s32[8,8,128]{2,1,0:T(8,128)} %amap_hbm.1, ...), custom_call_target="tpu_custom_call" | custom-call | tf_op jit(solution)/shard_map/pallas_call | solution.py:582
  23.3 0.7 %shard_map.95 = (f32[8,8,128]{2,1,0:T(8,128)}, f32[8,8,128]{2,1,0:T(8,128)}, f32[8,8,128]{2,1,0:T(8,128)}) custom-call(f32[8,8,128]{2,1,0:T(8,128)S(1)} %get-tuple-element.6.x_ref, f32[8,8,128]{2,1,0:T(8,128)S(1)} %get-tuple-element.7.r_ref, f32[8,8,128]{2,1,0:T(8,128)S(1)} %get-tuple-element.8.p_ref), custom_call_target="tpu_custom_call" | custom-call | tf_op jit(solution)/shard_map/pallas_call | solution.py:646

commit v3 on v2

--- a/solution.py
+++ b/solution.py
@@ -224,9 +224,11 @@
     def block_apply(picked_of, done_with_dot, first=False):
         dot = zero
         picked = picked_of(0)
+        if first:
+            for u in range(groups):
+                mat_copy(u).wait()
         for u in range(groups):
             if first:
-                mat_copy(u).wait()
                 for b in range(SUB):
                     high, low = split(mats[u * SUB + b])
                     pair, part = (u * SUB + b) // 2, pl.ds((b % 2) * LANES, LANES)

time: 24.1 us -> 23.2 us (0.963)
  Pallas kernels: 23.3 us -> 22.5 us
    pallas_call x1, Pallas kernels: 22.7 us -> 21.8 us  [shards(): pl.pallas_call(functools.partial(kernel, owners, members), out_shape=(fie...]
where the time goes in v3:
time: 23.2 us; the launch traced here: 23.1 us
  Pallas kernels  22.5 us (97%)
  between operations  0.64 us (3%)
    pallas_call x1, Pallas kernels, shards(): pl.pallas_call(functools.partial(kernel, owners, members), out_shape=(fie...  21.8 us
    pallas_call x1, Pallas kernels, shards(): pl.pallas_call(emit, out_shape=(field, field, field), in_specs=[vmem] * 3...  0.67 us

profile of v3, /device:TPU:0, one launch (start us, length us, event | category | flops | bytes accessed | tf_op | source)
XLA Modules:
  0.0 23.1 jit_solution(18405597109395720845)
XLA Ops:
  0.6 21.8 %shard_map.94 = (f32[8,8,128]{2,1,0:T(8,128)S(1)}, f32[8,8,128]{2,1,0:T(8,128)S(1)}, f32[8,8,128]{2,1,0:T(8,128)S(1)}) custom-call(f32[8,8,128]{2,1,0:T(8,128)} %r_hbm.1, s32[8,8,128]{2,1,0:T(8,128)} %cidx_hbm.1, f32[1,16]{1,0:T(1,128)} %bitcast.5, s32[8,8,128]{2,1,0:T(8,128)} %bitcast.4, f32[64,128,128]{2,1,0:T(8,128)} %bitcast.3, s32[8,8,128]{2,1,0:T(8,128)} %amap_hbm.1, ...), custom_call_target="tpu_custom_call" | custom-call | tf_op jit(solution)/shard_map/pallas_call | solution.py:584
  22.4 0.7 %shard_map.95 = (f32[8,8,128]{2,1,0:T(8,128)}, f32[8,8,128]{2,1,0:T(8,128)}, f32[8,8,128]{2,1,0:T(8,128)}) custom-call(f32[8,8,128]{2,1,0:T(8,128)S(1)} %get-tuple-element.6.x_ref, f32[8,8,128]{2,1,0:T(8,128)S(1)} %get-tuple-element.7.r_ref, f32[8,8,128]{2,1,0:T(8,128)S(1)} %get-tuple-element.8.p_ref), custom_call_target="tpu_custom_call" | custom-call | tf_op jit(solution)/shard_map/pallas_call | solution.py:648

commit v4 on v3

--- a/solution.py
+++ b/solution.py
@@ -39,7 +39,7 @@
     owners, members, r_hbm, cidx_hbm, table_hbm, cells_hbm, inv_ref, amap_hbm, diag_hbm,
     x_out, r_out, p_out,
     r_ref, cidx_ref, table_ref, cells_ref, amap_ref, diag_ref, in_sems,
-    mats, halves, rot, key_in, lane_in, key_out, lane_out, moved,
+    mats, highs, lows, rot, key_in, lane_in, key_out, lane_out, moved,
     first_ext, first_cols, first_corner_src, first_corners,
     w_ext, w_cols, w_corner_src, w_corners,
     b_ext, b_cols, b_corner_src, b_corners,
@@ -132,12 +132,12 @@
 
         for_all(one)
 
+    for u in range(groups):
+        mat_copy(u).start()
     for_near(
         lambda device: pl.semaphore_signal(barrier, inc=1, device_id=device, device_id_type=MESH)
     )
 
-    for u in range(groups):
-        mat_copy(u).start()
     for copy in in_copies:
         copy.wait()
 
@@ -175,7 +175,7 @@
 
     tall, taller, place = narrow(tall), narrow(taller), narrow(place & (LANES - 1))
     one, nothing = jnp.bfloat16(1), jnp.bfloat16(0)
-    found = jnp.zeros((2 * groups * SUB, LANES), jnp.float32)
+    parts = [jnp.zeros((2 * groups * SUB, LANES), jnp.float32)] * 2
     for g in range(groups):
         block = cells_ref[g]
         for b in range(0, SUB, 2):
@@ -188,10 +188,11 @@
             )
             column = narrow(jnp.bitwise_and(source, LANES - 1))
             right = jnp.where(taller == jnp.broadcast_to(column, taller.shape), one, nothing)
-            found = found + lax.dot_general(
+            at = (b // 2) % 2
+            parts[at] = parts[at] + lax.dot_general(
                 left, right, (((1,), (1,)), ((), ())), preferred_element_type=jnp.float32
             )
-    found = found.astype(jnp.int32)
+    found = jnp.maximum(parts[0], parts[1]).astype(jnp.int32)
     for g in range(groups):
         block = found[g * SUB : (g + 1) * SUB]
         spot = found[(groups + g) * SUB : (groups + g + 1) * SUB]
@@ -232,8 +233,8 @@
                 for b in range(SUB):
                     high, low = split(mats[u * SUB + b])
                     pair, part = (u * SUB + b) // 2, pl.ds((b % 2) * LANES, LANES)
-                    halves[pair, part, 0:LANES] = high
-                    halves[pair, part, LANES : 2 * LANES] = low
+                    highs[pair, part] = high
+                    lows[pair, part] = low
             upcoming = picked_of(u + 1) if u + 1 < groups else None
             sides = []
             for keep_odd in (False, True):
@@ -242,9 +243,9 @@
             left = jnp.concatenate(sides, axis=1)
             product = zero
             for j in range(SUB // 2):
-                both = jnp.dot(
-                    left, halves[u * SUB // 2 + j], preferred_element_type=jnp.float32
-                )
+                pair = u * SUB // 2 + j
+                right = jnp.concatenate([highs[pair], lows[pair]], axis=1)
+                both = jnp.dot(left, right, preferred_element_type=jnp.float32)
                 line = both[:SUB, :LANES] + (both[SUB:, :LANES] + both[:SUB, LANES:])
                 line = line + both[SUB:, LANES:]
                 product = jnp.where(lax.shift_right_logical(sub, 1) == j, line, product)
@@ -595,7 +596,8 @@
             pltpu.VMEM(coarse_diagonal.shape, f32),
             pltpu.SemaphoreType.DMA((6,)),
             pltpu.VMEM((blocks, side, side), f32),
-            pltpu.VMEM((blocks // 2, 2 * side, 2 * side), jnp.bfloat16),
+            pltpu.VMEM((blocks // 2, 2 * side, side), jnp.bfloat16),
+            pltpu.VMEM((blocks // 2, 2 * side, side), jnp.bfloat16),
             pltpu.VMEM((blocks,) + tile, f32),
             pltpu.VMEM((groups,) + tile, i32),
             pltpu.VMEM((groups,) + tile, i32),

time: 23.2 us -> 23.4 us (level)
  no operation moved by 1% of the time
where the time goes in v4:
time: 23.4 us; the launch traced here: 23.2 us
  Pallas kernels  22.6 us (97%)
  between operations  0.64 us (3%)
    pallas_call x1, Pallas kernels, shards(): pl.pallas_call(functools.partial(kernel, owners, members), out_shape=(fie...  21.9 us
    pallas_call x1, Pallas kernels, shards(): pl.pallas_call(emit, out_shape=(field, field, field), in_specs=[vmem] * 3...  0.67 us

profile of v4, /device:TPU:0, one launch (start us, length us, event | category | flops | bytes accessed | tf_op | source)
XLA Modules:
  0.0 23.2 jit_solution(2384081191621767163)
XLA Ops:
  0.6 21.9 %shard_map.94 = (f32[8,8,128]{2,1,0:T(8,128)S(1)}, f32[8,8,128]{2,1,0:T(8,128)S(1)}, f32[8,8,128]{2,1,0:T(8,128)S(1)}) custom-call(f32[8,8,128]{2,1,0:T(8,128)} %r_hbm.1, s32[8,8,128]{2,1,0:T(8,128)} %cidx_hbm.1, f32[1,16]{1,0:T(1,128)} %bitcast.5, s32[8,8,128]{2,1,0:T(8,128)} %bitcast.4, f32[64,128,128]{2,1,0:T(8,128)} %bitcast.3, s32[8,8,128]{2,1,0:T(8,128)} %amap_hbm.1, ...), custom_call_target="tpu_custom_call" | custom-call | tf_op jit(solution)/shard_map/pallas_call | solution.py:585
  22.6 0.7 %shard_map.95 = (f32[8,8,128]{2,1,0:T(8,128)}, f32[8,8,128]{2,1,0:T(8,128)}, f32[8,8,128]{2,1,0:T(8,128)}) custom-call(f32[8,8,128]{2,1,0:T(8,128)S(1)} %get-tuple-element.6.x_ref, f32[8,8,128]{2,1,0:T(8,128)S(1)} %get-tuple-element.7.r_ref, f32[8,8,128]{2,1,0:T(8,128)S(1)} %get-tuple-element.8.p_ref), custom_call_target="tpu_custom_call" | custom-call | tf_op jit(solution)/shard_map/pallas_call | solution.py:650

commit v5 on v4

--- a/solution.py
+++ b/solution.py
@@ -19,7 +19,6 @@
 MAIN = 8
 XLO, XHI, ZLO, ZHI, CORNER = 8, 9, 10, 11, 12
 SLOTS = 13
-REACH = SWEEPS
 DIRECTIONS = ((-1, 0), (1, 0), (0, -1), (0, 1), (-1, -1), (-1, 1), (1, -1), (1, 1))
 
 
@@ -87,22 +86,41 @@
     rows[...] = jnp.zeros(rows.shape, jnp.float32)
 
     barrier = pltpu.get_barrier_semaphore()
-    reach_o = max(REACH, -(-(owners - 1) // 3))
-    reach_m = max(REACH, -(-(members - 1) // 3))
-    low_o, high_o = jnp.maximum(o - reach_o, 0), jnp.minimum(o + reach_o, owners - 1) + 1
-    low_m, high_m = jnp.maximum(m - reach_m, 0), jnp.minimum(m + reach_m, members - 1) + 1
-    near = (high_o - low_o) * (high_m - low_m) - 1
-
-    def spans(size, reach):
-        return {min(at + reach, size - 1) - max(at - reach, 0) + 1 for at in range(size)}
-
+    step_o, step_m = -(-(owners - 1) // 3), -(-(members - 1) // 3)
+    reach = max(SWEEPS - 1, max(step_o - 1, 0) + max(step_m - 1, 0))
+
+    def height(away):
+        return reach - max(abs(away) - 1, 0) + 1
+
+    columns = [b for b in range(1 - members, members) if height(b) > 0]
+
+    def near_of(o, m, least, most):
+        total = -1
+        for b in columns:
+            size = most(o - height(b), 0, least(o + height(b), owners - 1))
+            total = total + size * ((m + b >= 0) & (m + b < members))
+        return total
+
+    near = near_of(
+        o, m, jnp.minimum, lambda low, zero, high: high - jnp.maximum(low, zero) + 1
+    )
     near_counts = sorted(
-        {a * b - 1 for a in spans(owners, reach_o) for b in spans(members, reach_m)}
+        {
+            near_of(at_o, at_m, min, lambda low, zero, high: high - max(low, zero) + 1)
+            for at_o in range(owners)
+            for at_m in range(members)
+        }
     )
 
     def other(d):
-        t = lax.rem(me + d, count)
-        return {"coarse": lax.div(t, members), "fine": lax.rem(t, members)}
+        if count & (count - 1) or members & (members - 1):
+            t = lax.rem(me + d, count)
+            return {"coarse": lax.div(t, members), "fine": lax.rem(t, members)}
+        t = (me + d) & (count - 1)
+        return {
+            "coarse": lax.shift_right_logical(t, members.bit_length() - 1),
+            "fine": t & (members - 1),
+        }
 
     def for_all(act):
         if count <= UNROLLED:
@@ -116,28 +134,37 @@
 
             lax.fori_loop(1, count, one, 0)
 
+    inside_m = {b: (m + b >= 0) & (m + b < members) for b in columns}
+
+    def greet_near(midway):
+        highest = min(reach + 1, owners - 1)
+        for a in range(-highest, highest + 1):
+            if a == 0:
+                midway()
+            inside_o = (o + a >= 0) & (o + a < owners)
+            for b in columns:
+                if (a or b) and abs(a) <= height(b):
+
+                    @pl.when(inside_o & inside_m[b])
+                    def _(a=a, b=b):
+                        pl.semaphore_signal(
+                            barrier, inc=1, device_id={"coarse": o + a, "fine": m + b},
+                            device_id_type=MESH,
+                        )
+
     def for_near(act):
         def one(device):
-            to_o, to_m = device["coarse"], device["fine"]
-            close = None
-            if reach_o < owners - 1:
-                close = (to_o >= low_o) & (to_o < high_o)
-            if reach_m < members - 1:
-                close_m = (to_m >= low_m) & (to_m < high_m)
-                close = close_m if close is None else close & close_m
-            if close is None:
-                act(device)
-            else:
-                pl.when(close)(functools.partial(act, device))
+            away_o, away_m = jnp.abs(device["coarse"] - o), jnp.abs(device["fine"] - m)
+            steps = jnp.maximum(away_o - 1, 0) + jnp.maximum(away_m - 1, 0)
+            pl.when(steps <= reach)(functools.partial(act, device))
 
         for_all(one)
 
-    for u in range(groups):
-        mat_copy(u).start()
-    for_near(
-        lambda device: pl.semaphore_signal(barrier, inc=1, device_id=device, device_id_type=MESH)
-    )
-
+    def load_matrices():
+        for u in range(groups):
+            mat_copy(u).start()
+
+    greet_near(load_matrices)
     for copy in in_copies:
         copy.wait()
 
@@ -222,13 +249,13 @@
         for g in range(groups):
             keep[g] = permuted(key_in[g], lane_in[g])
 
-    def block_apply(picked_of, done_with_dot, first=False):
+    def block_apply(picked_of, done_with_dot, first=False, hook_at=None, hook=None):
         dot = zero
         picked = picked_of(0)
-        if first:
-            for u in range(groups):
-                mat_copy(u).wait()
         for u in range(groups):
+            if first and u % (groups // 2) == 0:
+                for at in range(u, u + groups // 2):
+                    mat_copy(at).wait()
             if first:
                 for b in range(SUB):
                     high, low = split(mats[u * SUB + b])
@@ -236,6 +263,8 @@
                     highs[pair, part] = high
                     lows[pair, part] = low
             upcoming = picked_of(u + 1) if u + 1 < groups else None
+            if u == hook_at:
+                hook()
             sides = []
             for keep_odd in (False, True):
                 side = jnp.where(odd == keep_odd, picked, 0.0)
@@ -260,9 +289,11 @@
             moved[g] = permuted(key_out[g], lane_out[g])
         return [moved[g] for g in range(groups)]
 
-    def solve(values, done_with_dot=None):
+    def solve(values, done_with_dot, hook_at, hook):
         load_turns(values)
-        return block_apply(lambda g: permuted(key_in[g], lane_in[g]), done_with_dot)
+        return block_apply(
+            lambda g: permuted(key_in[g], lane_in[g]), done_with_dot, False, hook_at, hook
+        )
 
     base = lax.shift_right_logical(lane, 3)
 
@@ -285,9 +316,11 @@
             device_id=device, device_id_type=MESH,
         )
 
-    def send_rows(index, row, everywhere=False):
+    def put_row(index, row):
         row_src[index] = row[0:1, :]
         rows[index, me] = row[0:1, :]
+
+    def send_rows(index, everywhere=False):
         (for_all if everywhere else for_near)(
             lambda device: row_copy(index, row_src.at[index], rows.at[index, me], device).start()
         )
@@ -346,7 +379,7 @@
             )
         return copies
 
-    def start_halo(ring, fields, ext, cols, corner_src, corners):
+    def pack_halo(fields, cols, corner_src):
         packs = [zero, zero, zero, zero]
         for f, values in enumerate(fields):
             cols[0, f] = edge_rows(values, 0)
@@ -359,6 +392,8 @@
                     packs[at] = jnp.where(sub == f, full(values[x][z : z + 1, :]), packs[at])
         for at in range(4):
             corner_src[at] = packs[at]
+
+    def send_halo(ring, ext, cols, corner_src, corners):
         copies = halo_copies(ring, ext, cols, corner_src, corners)
         for goes, copy in copies:
             pl.when(goes)(copy.start)
@@ -443,44 +478,24 @@
     spread = pltpu.roll(spread, boxes, 1)
     first_row = restrict(start) + spread
     pick(start, picks)
-    pl.semaphore_wait(barrier, near)
-    send_rows(0, first_row)
+    put_row(0, first_row)
     kappas = [first_ext[x, 0] for x in range(MAIN)]
     maps = [first_ext[x, 1] for x in range(MAIN)]
-    start_halo(
-        0, [kappas, maps], first_ext, first_cols, first_corner_src, first_corners
-    )
+    pack_halo([kappas, maps], first_cols, first_corner_src)
+
+    def open_up():
+        pl.semaphore_wait(barrier, near)
+        send_rows(0)
+        send_halo(0, first_ext, first_cols, first_corner_src, first_corners)
+
+    late = (o >= owners - max(1, owners // 4)) & (m >= members // 2)
+    pl.when(late)(open_up)
     w = block_apply(lambda g: picks[g], None, True)
     for x in range(MAIN):
         w_ext[x, 0] = w[x]
-    start_halo(1, [w], w_ext, w_cols, w_corner_src, w_corners)
-    gathered = wait_rows(0)
-    inverse = only_boxes(pltpu.roll(gathered, LANES - boxes, 1))
-    guess = coarse_solve(only_boxes(gathered), inverse)
-
-    def guess_rows(guess):
-        picks = {}
-        for do in (-1, 0, 1):
-            for dm in (-1, 0, 1):
-                wanted = me + do * members + dm
-                picks[(do, dm)] = full(
-                    jnp.sum(jnp.where(node == wanted, guess, 0.0), axis=0, keepdims=True)
-                )
-        return picks
-
-    def add_coarse(values, guess):
-        picks = guess_rows(guess)
-        result = []
-        for x in range(MAIN):
-            result.append(values[x] + take(picks[(0, 0)], amaps[x]))
-        for slot, way in ((XLO, (-1, 0)), (XHI, (1, 0)), (ZLO, (0, -1)), (ZHI, (0, 1))):
-            result.append(values[slot] + take(picks[way], amaps[slot]))
-        corner = zero
-        for at, way in enumerate(((-1, -1), (-1, 1), (1, -1), (1, 1))):
-            corner = jnp.where(sub == at, take(picks[way], amaps[CORNER]), corner)
-        result.append(values[CORNER] + corner)
-        return result
-
+    pack_halo([w], w_cols, w_corner_src)
+    pl.when(jnp.logical_not(late))(open_up)
+    send_halo(1, w_ext, w_cols, w_corner_src, w_corners)
     wait_halo(0, 2)
     for slot in range(SLOTS):
         if slot == CORNER:
@@ -494,6 +509,33 @@
     for x in range(MAIN):
         kt[x] = 8.0 * kap[x] + smeared[x]
 
+    gathered = wait_rows(0)
+    inverse = only_boxes(pltpu.roll(gathered, LANES - boxes, 1))
+    guess = coarse_solve(only_boxes(gathered), inverse)
+
+    def guess_rows(guess):
+        picks = {}
+        for do in (-1, 0, 1):
+            for dm in (-1, 0, 1):
+                wanted = me + do * members + dm
+                picks[(do, dm)] = full(
+                    jnp.sum(jnp.where(node == wanted, guess, 0.0), axis=0, keepdims=True)
+                )
+        return picks
+
+    def coarse_parts(guess):
+        picks_of = guess_rows(guess)
+        result = []
+        for x in range(MAIN):
+            result.append(take(picks_of[(0, 0)], amaps[x]))
+        for slot, way in ((XLO, (-1, 0)), (XHI, (1, 0)), (ZLO, (0, -1)), (ZHI, (0, 1))):
+            result.append(take(picks_of[way], amaps[slot]))
+        corner = zero
+        for at, way in enumerate(((-1, -1), (-1, 1), (1, -1), (1, 1))):
+            corner = jnp.where(sub == at, take(picks_of[way], amaps[CORNER]), corner)
+        result.append(corner)
+        return result
+
     def arrived(ring, ext, corners):
         wait_halo(ring, 1)
         return [ext[s, 0] for s in range(CORNER)] + [corner_rows(corners, 0)]
@@ -504,20 +546,27 @@
         for x in range(MAIN):
             result[x] = field[x] * kt[x] - kap[x] * flat[x] - steep[x]
 
-    z = add_coarse(arrived(1, w_ext, w_corners), guess)
+    coarse = coarse_parts(guess)
+    z = [a + b for a, b in zip(arrived(1, w_ext, w_corners), coarse)]
     for slot in range(SLOTS):
         p_ext[slot] = z[slot]
     fine_operate(z, q_cur)
     image = [q_cur[x] for x in range(MAIN)]
-    send_rows(1, restrict(image))
-    bq = solve(image)
+    image_row = restrict(image)
+
+    def send_image():
+        put_row(1, image_row)
+        send_rows(1)
+
+    bq = solve(image, None, 0, send_image)
     for x in range(MAIN):
         b_ext[x, 0] = bq[x]
-    start_halo(2, [bq], b_ext, b_cols, b_corner_src, b_corners)
+    pack_halo([bq], b_cols, b_corner_src)
+    send_halo(2, b_ext, b_cols, b_corner_src, b_corners)
     r_dot_p = dot_of(r_ref, p_ext)
     p_dot_q = dot_of(p_ext, q_cur)
-    guess = coarse_solve(only_boxes(wait_rows(1)), inverse)
-    u = add_coarse(arrived(2, b_ext, b_corners), guess)
+    coarse = coarse_parts(coarse_solve(only_boxes(wait_rows(1)), inverse))
+    u = [a + b for a, b in zip(arrived(2, b_ext, b_corners), coarse)]
     for x in range(MAIN):
         u_ext[x] = u[x]
     fine_operate(u, v_cur)
@@ -527,8 +576,16 @@
     row = with_scalar(row, 1, p_dot_q)
     row = with_scalar(row, 2, dot_of(q_cur, u_ext))
     row = with_scalar(row, 3, dot_of(u_ext, v_cur))
-    send_rows(2, row, True)
-    bv = solve(image, lambda dot: send_rows(3, full(dot), True))
+
+    def send_moments():
+        put_row(2, row)
+        send_rows(2, True)
+
+    def send_last(dot):
+        put_row(3, full(dot))
+        send_rows(3, True)
+
+    bv = solve(image, send_last, groups // 2 - 1, send_moments)
     gathered = wait_rows(2, True)
     sums = jnp.sum(gathered, axis=0, keepdims=True)
     inverse = only_boxes(pltpu.roll(gathered, LANES - boxes, 1))

time: 23.4 us -> 22.9 us (0.979)
  Pallas kernels: 22.6 us -> 22.1 us
    pallas_call x1, Pallas kernels: 21.9 us -> 21.4 us  [shards(): pl.pallas_call(functools.partial(kernel, owners, members), out_shape=(fie...]
where the time goes in v5:
time: 22.9 us; the launch traced here: 22.7 us
  Pallas kernels  22.1 us (97%)
  between operations  0.64 us (3%)
    pallas_call x1, Pallas kernels, shards(): pl.pallas_call(functools.partial(kernel, owners, members), out_shape=(fie...  21.4 us
    pallas_call x1, Pallas kernels, shards(): pl.pallas_call(emit, out_shape=(field, field, field), in_specs=[vmem] * 3...  0.67 us

profile of v5, /device:TPU:0, one launch (start us, length us, event | category | flops | bytes accessed | tf_op | source)
XLA Modules:
  0.0 22.7 jit_solution(17068227160851210360)
XLA Ops:
  0.6 21.4 %shard_map.94 = (f32[8,8,128]{2,1,0:T(8,128)S(1)}, f32[8,8,128]{2,1,0:T(8,128)S(1)}, f32[8,8,128]{2,1,0:T(8,128)S(1)}) custom-call(f32[8,8,128]{2,1,0:T(8,128)} %r_hbm.1, s32[8,8,128]{2,1,0:T(8,128)} %cidx_hbm.1, f32[1,16]{1,0:T(1,128)} %bitcast.5, s32[8,8,128]{2,1,0:T(8,128)} %bitcast.4, f32[64,128,128]{2,1,0:T(8,128)} %bitcast.3, s32[8,8,128]{2,1,0:T(8,128)} %amap_hbm.1, ...), custom_call_target="tpu_custom_call" | custom-call | tf_op jit(solution)/shard_map/pallas_call | solution.py:642
  22.0 0.7 %shard_map.95 = (f32[8,8,128]{2,1,0:T(8,128)}, f32[8,8,128]{2,1,0:T(8,128)}, f32[8,8,128]{2,1,0:T(8,128)}) custom-call(f32[8,8,128]{2,1,0:T(8,128)S(1)} %get-tuple-element.6.x_ref, f32[8,8,128]{2,1,0:T(8,128)S(1)} %get-tuple-element.7.r_ref, f32[8,8,128]{2,1,0:T(8,128)S(1)} %get-tuple-element.8.p_ref), custom_call_target="tpu_custom_call" | custom-call | tf_op jit(solution)/shard_map/pallas_call | solution.py:707

commit v6 on v5

--- a/solution.py
+++ b/solution.py
@@ -10,6 +10,7 @@
 RINGS = 3
 ROUNDS = 4
 UNROLLED = 64
+WORD = 32
 SWEEPS = 4
 omega = 0.8
 restrict_scale = 0.25
@@ -152,19 +153,27 @@
                             device_id_type=MESH,
                         )
 
+    def is_near(device):
+        away_o, away_m = jnp.abs(device["coarse"] - o), jnp.abs(device["fine"] - m)
+        return jnp.maximum(away_o - 1, 0) + jnp.maximum(away_m - 1, 0) <= reach
+
     def for_near(act):
-        def one(device):
-            away_o, away_m = jnp.abs(device["coarse"] - o), jnp.abs(device["fine"] - m)
-            steps = jnp.maximum(away_o - 1, 0) + jnp.maximum(away_m - 1, 0)
-            pl.when(steps <= reach)(functools.partial(act, device))
-
-        for_all(one)
+        if count <= WORD:
+            for d in range(1, count):
+                pl.when((mask & (1 << (d - 1))) != 0)(functools.partial(act, other(d)))
+        else:
+            for_all(lambda device: pl.when(is_near(device))(functools.partial(act, device)))
 
     def load_matrices():
         for u in range(groups):
             mat_copy(u).start()
 
     greet_near(load_matrices)
+    mask = jnp.int32(0)
+    if count <= WORD:
+        for d in range(1, count):
+            mask = mask | (is_near(other(d)).astype(jnp.int32) << (d - 1))
+
     for copy in in_copies:
         copy.wait()
 

time: 22.9 us -> 22.7 us (level)
  no operation moved by 1% of the time
where the time goes in v6:
time: 22.7 us; the launch traced here: 22.5 us
  Pallas kernels  21.9 us (96%)
  between operations  0.64 us (3%)
    pallas_call x1, Pallas kernels, shards(): pl.pallas_call(functools.partial(kernel, owners, members), out_shape=(fie...  21.2 us
    pallas_call x1, Pallas kernels, shards(): pl.pallas_call(emit, out_shape=(field, field, field), in_specs=[vmem] * 3...  0.67 us

profile of v6, /device:TPU:0, one launch (start us, length us, event | category | flops | bytes accessed | tf_op | source)
XLA Modules:
  0.0 22.5 jit_solution(5637127060931768950)
XLA Ops:
  0.6 21.2 %shard_map.94 = (f32[8,8,128]{2,1,0:T(8,128)S(1)}, f32[8,8,128]{2,1,0:T(8,128)S(1)}, f32[8,8,128]{2,1,0:T(8,128)S(1)}) custom-call(f32[8,8,128]{2,1,0:T(8,128)} %r_hbm.1, s32[8,8,128]{2,1,0:T(8,128)} %cidx_hbm.1, f32[1,16]{1,0:T(1,128)} %bitcast.5, s32[8,8,128]{2,1,0:T(8,128)} %bitcast.4, f32[64,128,128]{2,1,0:T(8,128)} %bitcast.3, s32[8,8,128]{2,1,0:T(8,128)} %amap_hbm.1, ...), custom_call_target="tpu_custom_call" | custom-call | tf_op jit(solution)/shard_map/pallas_call | solution.py:651
  21.9 0.7 %shard_map.95 = (f32[8,8,128]{2,1,0:T(8,128)}, f32[8,8,128]{2,1,0:T(8,128)}, f32[8,8,128]{2,1,0:T(8,128)}) custom-call(f32[8,8,128]{2,1,0:T(8,128)S(1)} %get-tuple-element.6.x_ref, f32[8,8,128]{2,1,0:T(8,128)S(1)} %get-tuple-element.7.r_ref, f32[8,8,128]{2,1,0:T(8,128)S(1)} %get-tuple-element.8.p_ref), custom_call_target="tpu_custom_call" | custom-call | tf_op jit(solution)/shard_map/pallas_call | solution.py:716
